TPU v7x, 128 devices: a whole 4x4x4 slice. The times are simulated.
128 devices in a mesh: gx: 8 (over x, core), gy: 16 (over y, z).
Axes of the slice: x: 4, y: 4, z: 4, core: 2. Of those that a mesh axis runs over, the one named last changes fastest.
Arguments:
- off_state: float32 [5, 256, 256, 256], P(None, 'gx', 'gy'), may hold values from -0.9 to 3, as said below
- near_state: float32 [384, 5, 8, 64, 128], P(('gx', 'gy')), may hold values from -0.9 to 3, as said below
- near_metric: float32 [384, 3, 8, 64, 128], P(('gx', 'gy')), may hold values from 0.5 to 1.1
- slot_block: int32 [384], P(('gx', 'gy')), may hold values from -1 to 255, as said below
- block_faces: int32 [256, 2], replicated, may hold values from 0 to 255, as said below
- fringe_in: int32 [3, 1024], P(None, ('gx', 'gy')), may hold values from 0 to 23, as said below
- fringe_in_maps: bfloat16 [1024, 128, 128], P(('gx', 'gy')), may hold values from 0 to 1
- fringe_out: int32 [3, 1024], P(None, ('gx', 'gy')), may hold values from 0 to 23, as said below
- fringe_out_maps: bfloat16 [1024, 128, 128], P(('gx', 'gy')), may hold values from 0 to 1
Outputs:
- off_next: float32 [5, 256, 256, 256], P(None, 'gx', 'gy')
- near_next: float32 [384, 5, 8, 64, 128], P(('gx', 'gy'))
Inputs may be any that keep to these rules, and one draw needn't show every extreme that they name: `off_state`: component 0 (density) lies within 0.8 to 1.2, components 1 to 3 within -0.9 to 0.9, component 4 within 2 to 3. `near_state`: component 0 (density) lies within 0.8 to 1.2, components 1 to 3 within -0.9 to 0.9, component 4 within 2 to 3, in empty slots too. `slot_block`: entry 3 * d + s is the block in slot s of device d (devices in gx+gy order). A device's occupied slots come first and it holds at least one block; every block is in exactly one slot; the blocks of gx row r are numbered from r * 2 * 16 and held in that row; the devices at gy and gy + 8 of one row hold 4 blocks together. `block_faces`: row b gives the block across b's lower and upper face around the body; they agree (b is the lower neighbour of its upper neighbour) and lie in b's gx row. `fringe_in`: column 8 * d + k is row k of device d: entry 0 a near-body tile of d in an occupied slot, entry 1 the gy index of the receiving device in d's gx row, entry 2 one of its off-body tiles. Every off-body tile is replaced at most once; every device receives exactly 8 rows, and sends exactly 1 row to each of 8 devices. `fringe_out`: column 8 * d + k is row k of device d: entry 0 an off-body tile of d, entry 1 the gy index of the receiving device in d's gx row, entry 2 a near-body tile of that device in an occupied slot. Every near-body tile is replaced at most once; every device receives exactly 8 rows, and sends exactly 1 row to each of 8 devices.
All inputs are finite; a program needn't handle non-finite values.
Results may differ from a plain program's by a relative error of at most 0.0014.
The roundings to bfloat16 on the way count: a program that leaves them out, or rounds other values in their place, can miss the bound.
Values may be sent and summed in bfloat16 or wider, within the bound.
A program may use at most 384 MiB of HBM per device.

v0:
```python
import jax
import jax.numpy as jnp
from jax import lax
from jax.sharding import PartitionSpec as P

TW = 8
TL = 128
BLK_DEV = 2
FCAP = 1
BCAP = 3


HEAT_RATIO = 1.4
VISCOSITY = 0.8
CONDUCTION = 1.12
TIME_STEP = 0.1
WALL_SIGN = (1.0, -1.0, -1.0, -1.0, 1.0)
QUIET_STATE = (1.0, 0.0, 0.0, 0.0, 2.5)


def extended(block, sides, width):
    for axis, dim in sides:
        count = lax.axis_size(axis)
        forward = [(i, i + 1) for i in range(count - 1)]
        forward.append((count - 1, 0))
        backward = [(target, source) for source, target in forward]
        low = lax.ppermute(
            lax.slice_in_dim(block, block.shape[dim] - width, None, axis=dim), axis, forward
        )
        high = lax.ppermute(lax.slice_in_dim(block, 0, width, axis=dim), axis, backward)
        block = jnp.concatenate([low, block, high], axis=dim)
    return block


def as_sent(shard):

    def short(part):
        return part.astype(jnp.bfloat16) if part.dtype == jnp.float32 else part

    return jax.tree.map(short, shard)


def sent_to_all(shard, axis):
    copies = jnp.broadcast_to(shard, (lax.axis_size(axis), *shard.shape))
    return lax.all_to_all(copies, axis, split_axis=0, concat_axis=0, tiled=True)


def laid_out(pieces, dim):
    lengths = list(pieces.shape[1:])
    lengths[dim] *= pieces.shape[0]
    return jnp.moveaxis(pieces, 0, dim).reshape(lengths)


def collect(shard, axis, dim):
    pieces = sent_to_all(shard, axis)
    return laid_out(pieces, dim)


def in_blocks(shard, dim, size):
    before, after = (shard.shape[:dim], shard.shape[dim + 1 :])
    return jnp.moveaxis(shard.reshape(*before, size, -1, *after), dim, 0)


def piece_ends(length, count):
    unit = 8 if length >= 8 * count else 1
    return [length // unit * k // count * unit for k in range(1, count)]


def exchange_in_pieces(shard, axis, pieces, split_dim, concat_dim):
    blocks = in_blocks(shard, split_dim, lax.axis_size(axis))
    split_at = max(range(1, max(2, blocks.ndim - 1)), key=lambda d: blocks.shape[d])
    finished = []
    for slab in jnp.split(blocks, piece_ends(blocks.shape[split_at], pieces), axis=split_at):
        if slab.size:
            finished.append(lax.all_to_all(slab, axis, split_axis=0, concat_axis=0, tiled=True))
    return laid_out(jnp.concatenate(finished, axis=split_at), concat_dim)


def partner(value, axis, apart):
    mask = 2**apart
    pairs = [(source, source ^ mask) for source in range(lax.axis_size(axis))]
    return lax.ppermute(value, axis, pairs)


def shifted(values, direction, offset):
    leading = values.ndim - 3
    selector = [slice(None)] * leading
    for spatial in range(3):
        extent = values.shape[leading + spatial]
        if spatial == direction:
            selector.append(slice(1 + offset, extent - 1 + offset))
        else:
            selector.append(slice(1, extent - 1))
    return values[tuple(selector)]


def member(values, number):
    return values[..., number, :, :, :]


def residual(padded, metric):
    density = member(padded, 0)
    reciprocal_mass_per_volume = 1.0 / density
    fluid_speed_vector = [
        member(padded, 1 + direction) * reciprocal_mass_per_volume for direction in range(3)
    ]
    motion_work_share = 0.5 * (
        fluid_speed_vector[0] * fluid_speed_vector[0]
        + fluid_speed_vector[1] * fluid_speed_vector[1]
        + fluid_speed_vector[2] * fluid_speed_vector[2]
    )
    energy = member(padded, 4)
    normal_stress_level = (HEAT_RATIO - 1.0) * (energy - density * motion_work_share)
    thermal_level = normal_stress_level * reciprocal_mass_per_volume
    viscous_contribution = jnp.stack(
        [
            fluid_speed_vector[0],
            fluid_speed_vector[1],
            fluid_speed_vector[2],
            motion_work_share,
            thermal_level,
        ],
        axis=-4,
    )
    middle = shifted(viscous_contribution, 0, 0)
    summed = None
    for direction in range(3):
        momentum = member(padded, 1 + direction)
        pieces = [
            momentum,
            momentum * fluid_speed_vector[0],
            momentum * fluid_speed_vector[1],
            momentum * fluid_speed_vector[2],
            (energy + normal_stress_level) * fluid_speed_vector[direction],
        ]
        pieces[1 + direction] = pieces[1 + direction] + normal_stress_level
        fluxes = jnp.stack(pieces, axis=-4)
        difference = shifted(fluxes, direction, 1) - shifted(fluxes, direction, -1)
        second = (
            shifted(viscous_contribution, direction, 1)
            + shifted(viscous_contribution, direction, -1)
            - 2.0 * middle
        )
        viscous = jnp.stack(
            [
                jnp.zeros_like(member(second, 0)),
                VISCOSITY * member(second, 0),
                VISCOSITY * member(second, 1),
                VISCOSITY * member(second, 2),
                VISCOSITY * member(second, 3) + CONDUCTION * member(second, 4),
            ],
            axis=-4,
        )
        if metric is None:
            contrib = viscous - 0.5 * difference
        else:
            spacing = jnp.expand_dims(member(metric, direction), -4)
            contrib = spacing * spacing * viscous - 0.5 * spacing * difference
        summed = contrib if summed is None else summed + contrib
    return summed


def runge_kutta(initial, rate_of):
    section_one = initial + TIME_STEP * rate_of(initial)
    section_two = 0.75 * initial + 0.25 * (section_one + TIME_STEP * rate_of(section_one))
    return 1.0 / 3.0 * initial + 2.0 / 3.0 * (section_two + TIME_STEP * rate_of(section_two))


def frame_near(current, ghost_low, upper_ghost_cells):
    joined = jnp.concatenate([ghost_low, current, upper_ghost_cells], axis=3)
    wall_sign = jnp.array(WALL_SIGN, jnp.float32).reshape(5, 1, 1, 1)
    joined = jnp.concatenate([joined[:, :, 0:1] * wall_sign, joined, joined[:, :, -1:]], axis=2)
    return jnp.concatenate([joined[..., 0:1], joined, joined[..., -1:]], axis=4)


def off_tiles(fields):
    components, width_x, width_y, width_z = fields.shape
    blocks = fields.reshape(components, width_x // TW, TW, width_y // TW, TW, width_z // TL, TL)
    return blocks.transpose(1, 3, 5, 0, 2, 4, 6).reshape(-1, components * TW * TW * TL)


def off_fields(tiles, layout):
    components, width_x, width_y, width_z = layout
    blocks = tiles.reshape(width_x // TW, width_y // TW, width_z // TL, components, TW, TW, TL)
    return blocks.transpose(3, 0, 4, 1, 5, 2, 6).reshape(layout)


def near_tiles(fields):
    slots_here, components, normal, around, span_cells = fields.shape
    blocks = fields.reshape(slots_here, components, normal, around // TW, TW, span_cells)
    return blocks.transpose(0, 3, 1, 2, 4, 5).reshape(slots_here * (around // TW), -1)


def near_fields(tiles, layout):
    slots_here, components, normal, around, span_cells = layout
    blocks = tiles.reshape(slots_here, around // TW, components, normal, TW, span_cells)
    return blocks.transpose(0, 2, 3, 1, 4, 5).reshape(layout)


def off_hold(marks, layout):
    components, width_x, width_y, width_z = layout
    tile_grid = marks.reshape(width_x // TW, 1, width_y // TW, 1, width_z // TL, 1)
    spread = jnp.broadcast_to(tile_grid, (width_x // TW, TW, width_y // TW, TW, width_z // TL, TL))
    return 1.0 - spread.reshape(width_x, width_y, width_z)


def interpolate(tiles, chosen, tile_maps):
    donors = jnp.take(tiles, chosen, axis=0).astype(jnp.bfloat16)
    tile_lines = donors.reshape(donors.shape[0], -1, tile_maps.shape[-1])
    mixed_rows = jnp.einsum(
        "rkl,rlm->rkm", tile_lines, tile_maps, preferred_element_type=jnp.float32
    )
    return mixed_rows.astype(jnp.bfloat16).reshape(donors.shape[0], -1)


def bucketed(values, target_gy, target_tile, peer_count):
    row_total = values.shape[0]
    row_order = jnp.arange(row_total)
    before = (row_order[None, :] < row_order[:, None]) & (target_gy[None, :] == target_gy[:, None])
    rank_here = jnp.sum(before.astype(jnp.int32), axis=1)
    position = target_gy * FCAP + rank_here
    placing = jnp.arange(peer_count * FCAP)[:, None] == position[None, :]
    packed = jnp.dot(
        placing.astype(jnp.bfloat16), values, preferred_element_type=jnp.float32
    ).astype(jnp.bfloat16)
    labels = jnp.sum(jnp.where(placing, target_tile[None, :] + 1, 0), axis=1) - 1
    return (packed.reshape(peer_count, FCAP, -1), labels.reshape(peer_count, FCAP))


def settle(values, labels, tile_total):
    flat_values = values.reshape(-1, values.shape[-1])
    flat_labels = labels.reshape(-1)
    hit_table = jnp.arange(tile_total)[:, None] == flat_labels[None, :]
    placed = jnp.dot(
        hit_table.astype(jnp.bfloat16), flat_values, preferred_element_type=jnp.float32
    )
    return (placed, jnp.sum(hit_table.astype(jnp.float32), axis=1))


def neighbours(block_ids, block_faces):
    catalogue = jnp.arange(block_faces.shape[0])
    matches = block_ids[:, None] == catalogue[None, :]
    lower_ids = jnp.sum(jnp.where(matches, block_faces[None, :, 0], 0), axis=1)
    upper_ids = jnp.sum(jnp.where(matches, block_faces[None, :, 1], 0), axis=1)
    present = block_ids >= 0
    return (jnp.where(present, lower_ids, -1), jnp.where(present, upper_ids, -1))


def off_rate(fields, hold_mask):
    framed = extended(fields.astype(jnp.bfloat16), (("gx", 1), ("gy", 2)), 1).astype(fields.dtype)
    framed = jnp.concatenate([framed[..., -1:], framed, framed[..., :1]], axis=-1)
    return residual(framed, None) * hold_mask


def near_rate(fields, metric, hold_mask, block_ids, lower_ids, upper_ids):
    slots_here = fields.shape[0]
    face_cells = fields.shape[1] * fields.shape[2] * fields.shape[4]
    face_rows = jnp.concatenate([fields[:, :, :, 0, :], fields[:, :, :, -1, :]], axis=1)
    face_rows = face_rows.reshape(slots_here, 2 * face_cells)
    zeros_init = jnp.zeros((slots_here, face_cells), jnp.float32)
    portion_faces = collect(as_sent(face_rows), "gy", 0).astype(face_rows.dtype)
    portion_ids = collect(as_sent(block_ids), "gy", 0).astype(block_ids.dtype)
    from_lower = (portion_ids[None, :] == lower_ids[:, None]).astype(jnp.float32)
    from_upper = (portion_ids[None, :] == upper_ids[:, None]).astype(jnp.float32)
    ghost_low = zeros_init + jnp.dot(
        from_lower, portion_faces[:, face_cells:], precision=lax.Precision.HIGHEST
    )
    upper_ghost_cells = zeros_init + jnp.dot(
        from_upper, portion_faces[:, :face_cells], precision=lax.Precision.HIGHEST
    )
    ghost_low, upper_ghost_cells = (ghost_low, upper_ghost_cells)
    face_shape = (slots_here, fields.shape[1], fields.shape[2], 1, fields.shape[4])
    framed = frame_near(
        fields, ghost_low.reshape(face_shape), upper_ghost_cells.reshape(face_shape)
    )
    return residual(framed, metric) * hold_mask


def local(
    off_state,
    near_state,
    near_metric,
    slot_block,
    block_faces,
    fringe_in,
    fringe_in_maps,
    fringe_out,
    fringe_out_maps,
):
    occupied = slot_block >= 0
    quiet_state = jnp.array(QUIET_STATE, jnp.float32).reshape(1, 5, 1, 1, 1)
    near_filled = jnp.where(occupied[:, None, None, None, None], near_state, quiet_state)
    tiles_off = off_tiles(off_state)
    tiles_near = near_tiles(near_filled)
    count_off = tiles_off.shape[0]
    count_near = tiles_near.shape[0]
    sent_in = interpolate(tiles_near, fringe_in[0], fringe_in_maps)
    sent_out = interpolate(tiles_off, fringe_out[0], fringe_out_maps)
    peer_count = lax.axis_size("gy")
    packed_in, labels_in = bucketed(sent_in, fringe_in[1], fringe_in[2], peer_count)
    packed_out, labels_out = bucketed(sent_out, fringe_out[1], fringe_out[2], peer_count)
    arrived = (
        exchange_in_pieces(packed_in, "gy", 2, 0, 0),
        exchange_in_pieces(labels_in, "gy", 2, 0, 0),
        exchange_in_pieces(packed_out, "gy", 2, 0, 0),
        exchange_in_pieces(labels_out, "gy", 2, 0, 0),
    )
    got_off, marks_off = settle(arrived[0], arrived[1], count_off)
    got_near, marks_near = settle(arrived[2], arrived[3], count_near)
    tiles_off = jnp.where(marks_off[:, None] > 0.0, got_off, tiles_off)
    tiles_near = jnp.where(marks_near[:, None] > 0.0, got_near, tiles_near)
    off_start = off_fields(tiles_off, off_state.shape)
    hold_off = off_hold(marks_off, off_state.shape)
    off_next = runge_kutta(off_start, lambda fields: off_rate(fields, hold_off))
    near_start = near_fields(tiles_near, near_filled.shape)
    tile_hold = marks_near.reshape(near_filled.shape[0], -1)
    spare_slots = BCAP - BLK_DEV
    load_here = jnp.sum(occupied.astype(jnp.int32))
    partner_bit = lax.axis_size("gy").bit_length() - 2
    partner_parcel = partner(
        (near_start[BLK_DEV:], near_metric[BLK_DEV:], tile_hold[BLK_DEV:], slot_block[BLK_DEV:]),
        "gy",
        partner_bit,
    )
    work_seats = jnp.arange(BLK_DEV)
    keep_own = work_seats < load_here
    borrowed = jnp.clip(work_seats - load_here, 0, spare_slots - 1)

    def settle_work(own_part, partner_part):
        borrowed_rows = jnp.take(partner_part, borrowed, axis=0)
        keep_shape = keep_own.reshape((-1,) + (1,) * (own_part.ndim - 1))
        return jnp.where(keep_shape, own_part[:BLK_DEV], borrowed_rows)

    work_fields = settle_work(near_start, partner_parcel[0])
    work_metric = settle_work(near_metric, partner_parcel[1])
    work_hold = settle_work(tile_hold, partner_parcel[2])
    work_ids = settle_work(slot_block, partner_parcel[3])
    lower_ids, upper_ids = neighbours(work_ids, block_faces)
    hold_near = 1.0 - jnp.repeat(work_hold, TW, axis=1)[:, None, None, :, None]
    result = runge_kutta(
        work_fields,
        lambda fields: near_rate(fields, work_metric, hold_near, work_ids, lower_ids, upper_ids),
    )
    outward = jnp.clip(load_here + jnp.arange(spare_slots), 0, BLK_DEV - 1)
    returned = partner(jnp.take(result, outward, axis=0), "gy", partner_bit)
    merged = jnp.concatenate([result, returned], axis=0)
    near_next = jnp.where(occupied[:, None, None, None, None], merged, 0.0)
    return (off_next, near_next)


def solution(mesh):
    in_specs = (
        P(None, "gx", "gy", None),
        P(("gx", "gy"), None, None, None, None),
        P(("gx", "gy"), None, None, None, None),
        P(("gx", "gy")),
        P(),
        P(None, ("gx", "gy")),
        P(("gx", "gy"), None, None),
        P(None, ("gx", "gy")),
        P(("gx", "gy"), None, None),
    )
    out_specs = (P(None, "gx", "gy", None), P(("gx", "gy"), None, None, None, None))
    return jax.shard_map(local, mesh=mesh, in_specs=in_specs, out_specs=out_specs, check_vma=False)
```

profile of v0, /device:TPU:6, one launch (start us, length us, event | category | flops | bytes accessed | tf_op | source)
XLA Modules:
  0.0 860.2 jit_solution(13302194814976511811)
XLA Ops:
  3.6 8.0 all-to-all-start
  80.9 7.2 all-to-all-start.2
  104.1 11.5 %collective-permute-done.15 = f32[1,8]{1,0:T(1,128)S(1)} collective-permute-done((f32[1,8]{1,0:T(1,128)S(1)}, f32[1,8]{1,0:T(1,128)S(1)}, u32[]{:S(2)}, u32[]{:S(2)}) %collective-permute-start.15) | collective-permute-done | bytes 64 | tf_op jit(solution)/shard_map/ppermute | solution.py:82
  135.3 7.3 all-to-all-start.3
  153.4 8.2 collective-permute-done.3
  205.6 13.1 %fusion.246 = (bf16[5,32,16,256]{3,1,2,0:T(8,128)(2,1)S(1)}, f32[5,32,16,256]{3,1,2,0:T(8,128)}) fusion(f32[5,32,16,256]{3,1,2,0:T(8,128)S(1)} %bitcast.186, f32[32,16,256]{2,0,1:T(8,128)S(1)} %bitcast.197, f32[5,32,16,256]{3,1,2,0:T(8,128)S(1)} %copy-done.86, f32[5,34,18,258]{3,1,2,0:T(8,128)} %copy-done.64, f32[5,32,16,256]{3,1,2,0:T(8,128)S(1)} %copy-done.85, ...), kind=kLoop, calls=%fused_computation.675 | loop fusion | flops 9830400 | bytes 30670848 | tf_op jit(solution)/shard_map/convert_element_type | solution.py:250
  282.8 14.7 %fusion.244 = (bf16[5,32,16,256]{3,1,2,0:T(8,128)(2,1)S(1)}, f32[5,32,16,256]{3,1,2,0:T(8,128)}) fusion(f32[5,32,16,256]{3,1,2,0:T(8,128)S(1)} %copy-done.37, f32[32,16,256]{2,0,1:T(8,128)S(1)} %bitcast.198, f32[5,32,16,256]{3,1,2,0:T(8,128)} %fusion.174, f32[5,34,18,258]{3,1,2,0:T(8,128)} %copy-done.61, f32[5,32,16,256]{3,1,2,0:T(8,128)} %fusion.179, ...), kind=kLoop, calls=%fused_computation.674 | loop fusion | flops 11796480 | bytes 33292288 | tf_op jit(solution)/shard_map/convert_element_type | solution.py:250
  307.4 30.5 %collective-permute-done.11 = bf16[5,34,1,256]{3,1,2,0:T(8,128)(2,1)S(1)} collective-permute-done((bf16[5,34,1,256]{3,1,2,0:T(8,128)(2,1)S(1)}, bf16[5,34,1,256]{3,1,2,0:T(8,128)(2,1)S(1)}, u32[]{:S(2)}, u32[]{:S(2)}) %collective-permute-start.11) | collective-permute-done | bytes 87072 | tf_op jit(solution)/shard_map/ppermute | solution.py:30
  400.4 13.5 %pad_maximum_fusion = f32[2,5,10,66,130]{4,2,1,0,3:T(8,128)S(1)} fusion(f32[2,5,10,66,1]{4,2,1,0,3:T(8,128)} %get-tuple-element.185, f32[2,5,1,66,128]{4,2,1,0,3:T(1,128)S(1)} %get-tuple-element.197, f32[2,5,8,1,128]{4,2,1,0,3:T(8,128)S(1)} %bitcast.206, f32[2,5,8,64,128]{4,2,1,0,3:T(8,128)S(1)} %get-tuple-element.52, f32[2,5,8,1,128]{4,2,1,0,3:T(8,128)S(1)} %bitcast.218, ...), kind=kLoop, calls=%fused_computation.8 | loop fusion | flops 5148000 | bytes 6864000 | tf_op jit(solution)/shard_map/concatenate | solution.py:173
  433.7 24.9 %fusion.47 = (f32[2,5,8,64,128]{4,2,1,0,3:T(8,128)}, f32[2,5,8,64,128]{4,2,1,0,3:T(8,128)}, f32[2,5,8,64,128]{4,2,1,0,3:T(8,128)}) fusion(f32[2,5,10,66,130]{4,2,1,0,3:T(8,128)} %get-tuple-element.43), kind=kLoop, calls=%fused_computation.86 | loop fusion | flops 4587520 | bytes 26214400 | tf_op jit(solution)/shard_map/sub | solution.py:140
  466.9 7.6 add_dynamic-update-slice_fusion.8
  484.2 7.5 multiply_dynamic-update-slice_fusion.26
  499.1 22.6 %fusion.241 = (bf16[2,5,8,64,128]{4,2,1,0,3:T(8,128)(2,1)}, f32[2,5,8,64,128]{4,2,1,0,3:T(8,128)}) fusion(f32[2,5,8,64,128]{4,2,1,0,3:T(8,128)S(1)} %get-tuple-element.52, f32[2,64]{0,1:T(8,128)S(1)} %copy-done.88, f32[2,5,10,66,130]{4,2,1,0,3:T(8,128)} %get-tuple-element.95, f32[2,8,64,128]{3,1,0,2:T(8,128)S(1)} %copy-done.48, ...), kind=kLoop, calls=%fused_computation.672 | loop fusion | flops 11796480 | bytes 33292800 | tf_op jit(solution)/shard_map/convert.11
  554.6 13.5 %pad_maximum_fusion.1 = f32[2,5,10,66,130]{4,2,1,0,3:T(8,128)S(1)} fusion(f32[2,5,10,66,1]{4,2,1,0,3:T(8,128)} %get-tuple-element.183, f32[2,5,1,66,128]{4,2,1,0,3:T(1,128)S(1)} %get-tuple-element.195, f32[2,5,8,1,128]{4,2,1,0,3:T(8,128)S(1)} %bitcast.212, f32[2,5,8,64,128]{4,2,1,0,3:T(8,128)S(1)} %copy-done.7, f32[2,5,8,1,128]{4,2,1,0,3:T(8,128)S(1)} %bitcast.221, ...), kind=kLoop, calls=%fused_computation.9 | loop fusion | flops 5148000 | bytes 6864000 | tf_op jit(solution)/shard_map/concatenate | solution.py:173
  588.0 24.9 %fusion.33 = (f32[2,5,8,64,128]{4,2,1,0,3:T(8,128)}, f32[2,5,8,64,128]{4,2,1,0,3:T(8,128)}, f32[2,5,8,64,128]{4,2,1,0,3:T(8,128)}) fusion(f32[2,5,10,66,130]{4,2,1,0,3:T(8,128)} %get-tuple-element.33), kind=kLoop, calls=%fused_computation.65 | loop fusion | flops 4587520 | bytes 26214400 | tf_op jit(solution)/shard_map/sub | solution.py:140
  621.2 7.6 add_dynamic-update-slice_fusion.5
  638.4 7.5 multiply_dynamic-update-slice_fusion.16
  653.3 23.8 %fusion.239 = (bf16[2,5,8,64,128]{4,2,1,0,3:T(8,128)(2,1)}, f32[2,5,8,64,128]{4,2,1,0,3:T(8,128)}) fusion(f32[2,5,8,64,128]{4,2,1,0,3:T(8,128)} %get-tuple-element.42, f32[2,64]{0,1:T(8,128)S(1)} %copy-done.88, f32[2,5,10,66,130]{4,2,1,0,3:T(8,128)} %get-tuple-element.84, f32[2,8,64,128]{3,1,0,2:T(8,128)S(1)} %copy-done.48, ...), kind=kLoop, calls=%fused_computation.671 | loop fusion | flops 13762560 | bytes 35914240 | tf_op jit(solution)/shard_map/convert.5
  709.1 13.9 %pad_maximum_fusion.2 = f32[2,5,10,66,130]{4,2,1,0,3:T(8,128)S(1)} fusion(f32[2,5,10,66,1]{4,2,1,0,3:T(8,128)} %get-tuple-element.181, f32[2,5,1,66,128]{4,2,1,0,3:T(1,128)S(1)} %get-tuple-element.193, f32[2,5,8,1,128]{4,2,1,0,3:T(8,128)S(1)} %bitcast.209, f32[2,5,8,64,128]{4,2,1,0,3:T(8,128)S(1)} %copy-done.5, f32[2,5,8,1,128]{4,2,1,0,3:T(8,128)S(1)} %bitcast.215, ...), kind=kLoop, calls=%fused_computation.10 | loop fusion | flops 5148000 | bytes 6864000 | tf_op jit(solution)/shard_map/concatenate | solution.py:173
  757.4 7.4 multiply_dynamic-update-slice_fusion.6
  767.0 24.4 %fusion.17 = (f32[2,5,8,64,128]{4,2,1,0,3:T(8,128)}, f32[2,5,8,64,128]{4,2,1,0,3:T(8,128)}, f32[2,5,8,64,128]{4,2,1,0,3:T(8,128)S(1)}) fusion(f32[2,5,10,66,130]{4,2,1,0,3:T(8,128)} %get-tuple-element.23), kind=kLoop, calls=%fused_computation.42 | loop fusion | flops 4587520 | bytes 26214400 | tf_op jit(solution)/shard_map/sub | solution.py:140
  804.3 22.4 %fusion.9 = f32[2,5,8,64,128]{4,2,1,0,3:T(8,128)} fusion(f32[2,5,8,64,128]{4,2,1,0,3:T(8,128)S(1)} %copy-done.6, f32[2,5,10,66,130]{4,2,1,0,3:T(8,128)} %get-tuple-element.73, f32[2,5,10,66,130]{4,2,1,0,3:T(8,128)} %multiply_dynamic-update-slice_fusion.3, f32[2,5,10,66,130]{4,2,1,0,3:T(8,128)} %get-tuple-element.72, f32[2,5,8,64,128]{4,2,1,0,3:T(8,128)} %fusion.114, ...), kind=kLoop, calls=%fused_computation.28 | loop fusion | flops 13107200 | bytes 34603520 | tf_op jit(solution)/shard_map/add | solution.py:166
  831.6 14.0 %fusion.55 = f32[5,32,16,256]{3,1,2,0:T(8,128)S(1)} fusion(f32[5,32,16,256]{3,1,2,0:T(8,128)} %get-tuple-element.59, f32[5,32,16,256]{3,1,2,0:T(8,128)} %fusion.159, f32[5,34,18,258]{3,1,2,0:T(8,128)} %get-tuple-element.130, f32[5,32,16,256]{3,1,2,0:T(8,128)} %fusion.164, f32[5,34,18,258]{3,1,2,0:T(8,128)} %multiply_dynamic-update-slice_fusion.33, ...), kind=kLoop, calls=%fused_computation.96 | loop fusion | flops 11141120 | bytes 31981568 | tf_op jit(solution)/shard_map/add | solution.py:166
  848.5 8.5 collective-permute-done.16
  (536 shorter events, 512.5 us)
Async XLA Ops:
  3.6 77.3 %all-to-all-start = ((s32[16,1,1]{2,1,0:T(1,128)}), s32[16,1,1]{2,1,0:T(1,128)S(1)}, u32[]{:S(2)}, u32[]{:S(2)}) async-start(s32[16,1,1]{2,1,0:T(1,128)} %copy.93), calls=%async_computation | async-start | bytes 16384 | tf_op jit(solution)/shard_map/all_to_all | solution.py:75
  12.9 65.3 %collective-permute-start.14 = (s32[1]{0:T(128)}, s32[1]{0:T(128)}, u32[]{:S(2)}, u32[]{:S(2)}) collective-permute-start(s32[1]{0:T(128)} %slice.958), channel_id=1, source_target_pairs={{0,8},{1,9},{2,10},{3,11},{4,12},{5,13},{6,14},{7,15},{8,0},{9,1},... | collective-permute-start | bytes 20 | tf_op jit(solution)/shard_map/ppermute | solution.py:82
  18.4 131.9 %collective-permute-start.13 = (f32[1,3,8,64,128]{4,3,2,1,0:T(8,128)}, f32[1,3,8,64,128]{4,3,2,1,0:T(8,128)}, u32[]{:S(2)}, u32[]{:S(2)}) collective-permute-start(f32[1,3,8,64,128]{4,3,2,1,0:T(8,128)} %slice.955), channel_id=1, source_target_pairs={{0,8},{1,9},{2,10},{3,11},{4,12},{5,13},{6,14},{7,15},{8,0},{9,1},... | collective-permute-start | bytes 2359304 | tf_op jit(solution)/shard_map/ppermute | solution.py:82
  80.9 14.8 %all-to-all-start.2 = ((s32[16,1,1]{2,1,0:T(1,128)}), s32[16,1,1]{2,1,0:T(1,128)S(1)}, u32[]{:S(2)}, u32[]{:S(2)}) async-start(s32[16,1,1]{2,1,0:T(1,128)} %copy.101), calls=%async_computation.2 | async-start | bytes 16384 | tf_op jit(solution)/shard_map/all_to_all | solution.py:75
  95.7 22.3 %all-to-all-start.1 = ((bf16[16,2,20480]{2,1,0:T(2,128)(2,1)}), bf16[16,2,20480]{2,1,0:T(2,128)(2,1)}, u32[]{:S(2)}, u32[]{:S(2)}) async-start(bf16[16,2,20480]{2,1,0:T(2,128)(2,1)} %reshape.360), calls=%async_computation.1 | async-start | bytes 2621440 | tf_op jit(solution)/shard_map/all_to_all | solution.py:75
  100.8 14.8 %collective-permute-start.15 = (f32[1,8]{1,0:T(1,128)S(1)}, f32[1,8]{1,0:T(1,128)S(1)}, u32[]{:S(2)}, u32[]{:S(2)}) collective-permute-start(f32[1,8]{1,0:T(1,128)S(1)} %slice_bitcast_fusion.8), channel_id=1, source_target_pairs={{0,8},{1,9},{2,10},{3,11},{4,12},{5,13},{6,14},{7,15},{8,0},{9,1},... | collective-permute-start | bytes 104 | tf_op jit(solution)/shard_map/ppermute | solution.py:82
  118.6 16.7 %all-to-all-start.4 = ((s32[16,1,2]{2,1,0:T(1,128)}), s32[16,1,2]{2,1,0:T(1,128)S(1)}, u32[]{:S(2)}, u32[]{:S(2)}) async-start(s32[16,1,2]{2,1,0:T(1,128)} %broadcast_in_dim.239), calls=%async_computation.4 | async-start | bytes 16384 | tf_op jit(solution)/shard_map/all_to_all | solution.py:45
  134.2 9.7 %collective-permute-start.1 = (bf16[5,1,16,256]{3,1,2,0:T(2,128)(2,1)S(1)}, bf16[5,1,16,256]{3,1,2,0:T(2,128)(2,1)S(1)}, u32[]{:S(2)}, u32[]{:S(2)}) collective-permute-start(bf16[5,1,16,256]{3,1,2,0:T(2,128)(2,1)S(1)} %get-tuple-element.224), channel_id=1, source_target_pairs={{16,0},{32,16},{48,32},{64,48},{80,64},{96,80},{112,96},{0,112},{1... | collective-permute-start | bytes 122888 | tf_op jit(solution)/shard_map/ppermute | solution.py:30
  134.2 9.7 %collective-permute-start = (bf16[5,1,16,256]{3,1,2,0:T(2,128)(2,1)S(1)}, bf16[5,1,16,256]{3,1,2,0:T(2,128)(2,1)S(1)}, u32[]{:S(2)}, u32[]{:S(2)}) collective-permute-start(bf16[5,1,16,256]{3,1,2,0:T(2,128)(2,1)S(1)} %get-tuple-element.223), channel_id=1, source_target_pairs={{0,16},{16,32},{32,48},{48,64},{64,80},{80,96},{96,112},{112,0},{1... | collective-permute-start | bytes 122888 | tf_op jit(solution)/shard_map/ppermute | solution.py:27
  135.3 91.2 %all-to-all-start.3 = ((bf16[16,2,20480]{2,1,0:T(2,128)(2,1)}), bf16[16,2,20480]{2,1,0:T(2,128)(2,1)}, u32[]{:S(2)}, u32[]{:S(2)}) async-start(bf16[16,2,20480]{2,1,0:T(2,128)(2,1)} %reshape.362), calls=%async_computation.3 | async-start | bytes 2621440 | tf_op jit(solution)/shard_map/all_to_all | solution.py:75
  145.0 16.7 %collective-permute-start.3 = (bf16[5,34,1,256]{3,1,2,0:T(8,128)(2,1)S(1)}, bf16[5,34,1,256]{3,1,2,0:T(8,128)(2,1)S(1)}, u32[]{:S(2)}, u32[]{:S(2)}) collective-permute-start(bf16[5,34,1,256]{3,1,2,0:T(8,128)(2,1)S(1)} %get-tuple-element.212), channel_id=1, source_target_pairs={{1,0},{2,1},{3,2},{4,3},{5,4},{6,5},{7,6},{8,7},{9,8},{10,9},{11,1... | collective-permute-start | bytes 261128 | tf_op jit(solution)/shard_map/ppermute | solution.py:30
  150.3 15.3 %collective-permute-start.2 = (bf16[5,34,1,256]{3,1,2,0:T(8,128)(2,1)S(1)}, bf16[5,34,1,256]{3,1,2,0:T(8,128)(2,1)S(1)}, u32[]{:S(2)}, u32[]{:S(2)}) collective-permute-start(bf16[5,34,1,256]{3,1,2,0:T(8,128)(2,1)S(1)} %get-tuple-element.211), channel_id=1, source_target_pairs={{0,1},{1,2},{2,3},{3,4},{4,5},{5,6},{6,7},{7,8},{8,9},{9,10},{10,1... | collective-permute-start | bytes 261128 | tf_op jit(solution)/shard_map/ppermute | solution.py:27
  218.8 13.7 %collective-permute-start.5 = (bf16[5,1,16,256]{3,1,2,0:T(2,128)(2,1)S(1)}, bf16[5,1,16,256]{3,1,2,0:T(2,128)(2,1)S(1)}, u32[]{:S(2)}, u32[]{:S(2)}) collective-permute-start(bf16[5,1,16,256]{3,1,2,0:T(2,128)(2,1)S(1)} %get-tuple-element.222), channel_id=1, source_target_pairs={{16,0},{32,16},{48,32},{64,48},{80,64},{96,80},{112,96},{0,112},{1... | collective-permute-start | bytes 122888 | tf_op jit(solution)/shard_map/ppermute | solution.py:30
  219.3 13.2 %collective-permute-start.4 = (bf16[5,1,16,256]{3,1,2,0:T(2,128)(2,1)S(1)}, bf16[5,1,16,256]{3,1,2,0:T(2,128)(2,1)S(1)}, u32[]{:S(2)}, u32[]{:S(2)}) collective-permute-start(bf16[5,1,16,256]{3,1,2,0:T(2,128)(2,1)S(1)} %get-tuple-element.221), channel_id=1, source_target_pairs={{0,16},{16,32},{32,48},{48,64},{64,80},{80,96},{96,112},{112,0},{1... | collective-permute-start | bytes 122888 | tf_op jit(solution)/shard_map/ppermute | solution.py:27
  233.5 9.8 %collective-permute-start.7 = (bf16[5,34,1,256]{3,1,2,0:T(8,128)(2,1)S(1)}, bf16[5,34,1,256]{3,1,2,0:T(8,128)(2,1)S(1)}, u32[]{:S(2)}, u32[]{:S(2)}) collective-permute-start(bf16[5,34,1,256]{3,1,2,0:T(8,128)(2,1)S(1)} %get-tuple-element.210), channel_id=1, source_target_pairs={{1,0},{2,1},{3,2},{4,3},{5,4},{6,5},{7,6},{8,7},{9,8},{10,9},{11,1... | collective-permute-start | bytes 261128 | tf_op jit(solution)/shard_map/ppermute | solution.py:30
  235.5 9.2 %collective-permute-start.6 = (bf16[5,34,1,256]{3,1,2,0:T(8,128)(2,1)S(1)}, bf16[5,34,1,256]{3,1,2,0:T(8,128)(2,1)S(1)}, u32[]{:S(2)}, u32[]{:S(2)}) collective-permute-start(bf16[5,34,1,256]{3,1,2,0:T(8,128)(2,1)S(1)} %get-tuple-element.209), channel_id=1, source_target_pairs={{0,1},{1,2},{2,3},{3,4},{4,5},{5,6},{6,7},{7,8},{8,9},{9,10},{10,1... | collective-permute-start | bytes 261128 | tf_op jit(solution)/shard_map/ppermute | solution.py:27
  297.8 3.9 collective-permute-start.8
  301.7 36.3 %collective-permute-start.11 = (bf16[5,34,1,256]{3,1,2,0:T(8,128)(2,1)S(1)}, bf16[5,34,1,256]{3,1,2,0:T(8,128)(2,1)S(1)}, u32[]{:S(2)}, u32[]{:S(2)}) collective-permute-start(bf16[5,34,1,256]{3,1,2,0:T(8,128)(2,1)S(1)} %get-tuple-element.208), channel_id=1, source_target_pairs={{1,0},{2,1},{3,2},{4,3},{5,4},{6,5},{7,6},{8,7},{9,8},{10,9},{11,1... | collective-permute-start | bytes 261128 | tf_op jit(solution)/shard_map/ppermute | solution.py:30
  306.7 36.7 %collective-permute-start.10 = (bf16[5,34,1,256]{3,1,2,0:T(8,128)(2,1)S(1)}, bf16[5,34,1,256]{3,1,2,0:T(8,128)(2,1)S(1)}, u32[]{:S(2)}, u32[]{:S(2)}) collective-permute-start(bf16[5,34,1,256]{3,1,2,0:T(8,128)(2,1)S(1)} %get-tuple-element.207), channel_id=1, source_target_pairs={{0,1},{1,2},{2,3},{3,4},{4,5},{5,6},{6,7},{7,8},{8,9},{9,10},{10,1... | collective-permute-start | bytes 261128 | tf_op jit(solution)/shard_map/ppermute | solution.py:27
  306.9 62.2 %collective-permute-start.12 = (f32[1,5,8,64,128]{4,3,2,1,0:T(8,128)S(1)}, f32[1,5,8,64,128]{4,3,2,1,0:T(8,128)S(1)}, u32[]{:S(2)}, u32[]{:S(2)}) collective-permute-start(f32[1,5,8,64,128]{4,3,2,1,0:T(8,128)S(1)} %slice_bitcast_fusion.1), channel_id=1, source_target_pairs={{0,8},{1,9},{2,10},{3,11},{4,12},{5,13},{6,14},{7,15},{8,0},{9,1},... | collective-permute-start | bytes 3932168 | tf_op jit(solution)/shard_map/ppermute | solution.py:82
  372.8 16.7 %all-to-all-start.5 = ((bf16[16,2,10240]{2,1,0:T(2,128)(2,1)}), bf16[16,2,10240]{2,1,0:T(2,128)(2,1)S(1)}, u32[]{:S(2)}, u32[]{:S(2)}) async-start(bf16[16,2,10240]{2,1,0:T(2,128)(2,1)} %broadcast_in_dim.244), calls=%async_computation.5 | async-start | bytes 1310720 | tf_op jit(solution)/shard_map/all_to_all | solution.py:45
  523.7 16.2 %all-to-all-start.6 = ((bf16[16,2,10240]{2,1,0:T(2,128)(2,1)}), bf16[16,2,10240]{2,1,0:T(2,128)(2,1)}, u32[]{:S(2)}, u32[]{:S(2)}) async-start(bf16[16,2,10240]{2,1,0:T(2,128)(2,1)} %broadcast_in_dim.250), calls=%async_computation.6 | async-start | bytes 1310720 | tf_op jit(solution)/shard_map/all_to_all | solution.py:45
  679.1 15.3 %all-to-all-start.7 = ((bf16[16,2,10240]{2,1,0:T(2,128)(2,1)}), bf16[16,2,10240]{2,1,0:T(2,128)(2,1)}, u32[]{:S(2)}, u32[]{:S(2)}) async-start(bf16[16,2,10240]{2,1,0:T(2,128)(2,1)} %broadcast_in_dim.251), calls=%async_computation.7 | async-start | bytes 1310720 | tf_op jit(solution)/shard_map/all_to_all | solution.py:45
  828.3 28.7 %collective-permute-start.16 = (f32[1,5,8,64,128]{4,2,1,0,3:T(8,128)S(1)}, f32[1,5,8,64,128]{4,2,1,0,3:T(8,128)S(1)}, u32[]{:S(2)}, u32[]{:S(2)}) collective-permute-start(f32[1,5,8,64,128]{4,2,1,0,3:T(8,128)S(1)} %dynamic-slice_select_fusion), channel_id=1, source_target_pairs={{0,8},{1,9},{2,10},{3,11},{4,12},{5,13},{6,14},{7,15},{8,0},{9,1},... | collective-permute-start | bytes 3932168 | tf_op jit(solution)/shard_map/ppermute | solution.py:82
  (108 other events, 881.7 us)
where the time goes:
time: 872 us; the launch traced here: 860 us
  other arithmetic  525 us (60%)
  local copies, waits for them, and re-layouts  146 us (17%)
  waiting for transfers between devices  98.7 us (11%)
  starting transfers between devices  66.2 us (8%)
  matrix products  21.8 us (2%)
    unnamed x92, other arithmetic  162 us
    sub x6, other arithmetic, residual(): shifted(viscous_contribution, direction, 1)  93.6 us
    unnamed x255, local copies, waits for them, and re-layouts  83.2 us
    another operation x3, other arithmetic  48 us
    concatenate x3, other arithmetic, frame_near(): return jnp.concatenate([joined[..., 0:1], joined, joined[..., -1:]], axis=4)  41 us
    ppermute x6, waiting for transfers between devices, extended(): lax.ppermute(lax.slice_in_dim(block, 0, width, axis=dim), axis, backward)  40.1 us
    another operation x12, other arithmetic, residual(): fluxes = jnp.stack(pieces, axis=-4)  39 us
    add x2, other arithmetic, runge_kutta(): 1.0 / 3.0 * initial  36.4 us
  transfers between devices with their start and end apart: 25, of which 14 were waited for; matrix products, arithmetic and copies ran while one was open for 24% of the time, Pallas kernels for 0%

commit v1 on v0

v1 whole, which is shorter than its diff:
```python
import functools

import jax
import jax.numpy as jnp
from jax import lax
from jax.experimental import pallas as pl
from jax.experimental.pallas import tpu as pltpu
from jax.sharding import PartitionSpec as P

MESH = pl.DeviceIdType.MESH
F32 = jnp.float32
BF16 = jnp.bfloat16

TW = 8
TL = 128
BCAP = 3
NROW = 8
NT_OFF = 16
NT_NEAR = 24
PEERS = 16
DT = 0.1
RK = ((0.0, 1.0), (0.75, 0.25), (1.0 / 3.0, 2.0 / 3.0))

TXX, TXY, TXZ, TYY, TYZ, HX, HY, VX, VY, VZ, Q, MX, MY = range(13)
XF = (MX, TXX, TXY, TXZ, HX)
YF = (MY, TXY, TYY, TYZ, HY)
VF = (VX, VY, VZ, Q)
XK = XF + VF
YK = YF + VF

S_OFF, S_NEAR, S_LO, S_HI, S_OCC = 0, 16, 40, 43, 46


def primitives(u):
    rho, mx, my, mz, en = u
    r = 1.0 / rho
    vx, vy, vz = mx * r, my * r, mz * r
    mv = mx * vx + my * vy + mz * vz
    p = 0.4 * en - 0.2 * mv
    q = r * (0.5 * mv + 1.4 * p)
    return vx, vy, vz, p, q, en + p


def x_terms(u):
    vx, vy, vz, p, q, h = primitives(u)
    mx = u[1]
    return (mx, mx * vx + p, mx * vy, mx * vz, h * vx, vx, vy, vz, q)


def y_terms(u):
    vx, vy, vz, p, q, h = primitives(u)
    my = u[2]
    return (my, my * vx, my * vy + p, my * vz, h * vy, vx, vy, vz, q)


def interp_kernel(fin, fout, off, near, maps_in, maps_out, send, buf_in, buf_out, sems):
    copies = []
    for k in range(NROW):
        t = fin[0, k]
        copies.append(
            pltpu.make_async_copy(
                near.at[t // 8, :, :, pl.ds(pl.multiple_of((t % 8) * 8, 8), 8), :],
                buf_in.at[k],
                sems.at[0, k],
            )
        )
        t = fout[0, k]
        copies.append(
            pltpu.make_async_copy(
                off.at[
                    :,
                    pl.ds((t // 4) * 8, 8),
                    pl.ds(pl.multiple_of(((t // 2) % 2) * 8, 8), 8),
                    pl.ds(pl.multiple_of((t % 2) * 128, 128), 128),
                ],
                buf_out.at[k],
                sems.at[1, k],
            )
        )
    for c in copies:
        c.start()
    for k in range(NROW):
        for d, (buf, maps, tab) in enumerate(((buf_in, maps_in, fin), (buf_out, maps_out, fout))):
            copies[2 * k + d].wait()
            x = buf[k].reshape(320, 128).astype(BF16)
            y = jnp.dot(x, maps[k], preferred_element_type=F32)
            send[d, tab[1, k]] = y.astype(BF16)


def interpolate(fringe_in, fringe_out, off_state, near_state, maps_in, maps_out):
    return pl.pallas_call(
        interp_kernel,
        out_shape=jax.ShapeDtypeStruct((2, PEERS, 320, 128), BF16),
        in_specs=[
            pl.BlockSpec(memory_space=pltpu.SMEM),
            pl.BlockSpec(memory_space=pltpu.SMEM),
            pl.BlockSpec(memory_space=pl.ANY),
            pl.BlockSpec(memory_space=pl.ANY),
            pl.BlockSpec(memory_space=pltpu.VMEM),
            pl.BlockSpec(memory_space=pltpu.VMEM),
        ],
        out_specs=pl.BlockSpec(memory_space=pltpu.VMEM),
        scratch_shapes=[
            pltpu.VMEM((NROW, 5, 8, 8, 128), F32),
            pltpu.VMEM((NROW, 5, 8, 8, 128), F32),
            pltpu.SemaphoreType.DMA((2, NROW)),
        ],
        compiler_params=pltpu.CompilerParams(vmem_limit_bytes=24 << 20),
        name="interp",
    )(fringe_in, fringe_out, off_state, near_state, maps_in, maps_out)


def main_kernel(
    tab,
    off,
    near,
    metric,
    send,
    zoff,
    znear,
    off_out,
    near_out,
    u0o,
    u0n,
    uo,
    un,
    met,
    so,
    sn,
    rzo,
    rzn,
    recv,
    fsend,
    frecv0,
    frecv1,
    frecv2,
    xrecv,
    ysend,
    yrecv,
    go,
    gn,
    load_sem,
    out_sem,
    fr_send,
    fr_recv,
    fc_send,
    fc_recv,
    hx_send,
    hx_recv,
    hy_send,
    hy_recv,
):
    frecv = (frecv0, frecv1, frecv2)
    gx = lax.axis_index("gx")
    gy = lax.axis_index("gy")
    nx = 8
    peers = [lax.rem(gy + d, PEERS) for d in range(1, PEERS)]
    xup, xdn = lax.rem(gx + 1, nx), lax.rem(gx + nx - 1, nx)
    yup, ydn = lax.rem(gy + 1, PEERS), lax.rem(gy + PEERS - 1, PEERS)

    loads = [
        pltpu.make_async_copy(off.at[:, :, pl.ds(0, 128)], u0o.at[0], load_sem.at[0]),
        pltpu.make_async_copy(off.at[:, :, pl.ds(128, 128)], u0o.at[1], load_sem.at[1]),
        pltpu.make_async_copy(near, u0n, load_sem.at[2]),
        pltpu.make_async_copy(metric, met, load_sem.at[3]),
    ]
    for c in loads:
        c.start()

    barrier = pltpu.get_barrier_semaphore()
    for p in peers:
        pl.semaphore_signal(barrier, inc=1, device_id=(gx, p), device_id_type=MESH)
    for p in (xup, xdn):
        pl.semaphore_signal(barrier, inc=1, device_id=(p, gy), device_id_type=MESH)
    pl.semaphore_wait(barrier, PEERS + 1)

    fringe = []
    for d in range(2):
        for i, p in enumerate(peers):
            fringe.append(
                pltpu.make_async_remote_copy(
                    send.at[d, p],
                    recv.at[d, gy],
                    fr_send.at[d, i],
                    fr_recv.at[d, i],
                    device_id=(gx, p),
                    device_id_type=MESH,
                )
            )
    own = [
        pltpu.make_async_copy(send.at[d, gy], recv.at[d, gy], fr_send.at[d, PEERS - 1])
        for d in range(2)
    ]
    for c in own + fringe:
        c.start()
    for c in loads:
        c.wait()
    for c in own:
        c.wait()
    for c in fringe:
        c.wait_send()
        c.wait_recv()

    def settle_off(t, _):
        src = tab[S_OFF + t]
        take = src >= 0
        at = jnp.maximum(src, 0)
        half = lax.rem(t, 2)
        base = (t // 4) * 128 + lax.rem(t // 2, 2) * 8
        for c in range(5):
            for a in range(4):
                v = recv[0, at, pl.ds(c * 64 + a * 16, 16), :].astype(F32)
                for b in range(2):
                    rows = pl.ds(pl.multiple_of(base + (2 * a + b) * 16, 8), 8)
                    old = u0o[half, c, rows, :]
                    u0o[half, c, rows, :] = jnp.where(take, v[8 * b : 8 * b + 8], old)
        return 0

    def settle_near(t, _):
        src = tab[S_NEAR + t]
        take = src >= 0
        at = jnp.maximum(src, 0)
        s = t // 8
        base = lax.rem(t, 8) * 8
        for c in range(5):
            for a in range(4):
                v = recv[1, at, pl.ds(c * 64 + a * 16, 16), :].astype(F32)
                for b in range(2):
                    rows = pl.ds(pl.multiple_of(base + (2 * a + b) * 64, 8), 8)
                    old = u0n[s, c, rows, :]
                    u0n[s, c, rows, :] = jnp.where(take, v[8 * b : 8 * b + 8], old)
        return 0

    lax.fori_loop(0, NT_OFF, settle_off, 0)
    lax.fori_loop(0, NT_NEAR, settle_near, 0)

    def halo_copies(st, u):
        return (
            pltpu.make_async_remote_copy(
                u.at[:, :, pl.ds(0, 16), :], xrecv.at[st, 1], hx_send.at[st, 0], hx_recv.at[st, 1],
                device_id=(xdn, gy), device_id_type=MESH,
            ),
            pltpu.make_async_remote_copy(
                u.at[:, :, pl.ds(496, 16), :], xrecv.at[st, 0], hx_send.at[st, 1], hx_recv.at[st, 0],
                device_id=(xup, gy), device_id_type=MESH,
            ),
            pltpu.make_async_remote_copy(
                ysend.at[st, 0], yrecv.at[st, 1], hy_send.at[st, 0], hy_recv.at[st, 1],
                device_id=(gx, ydn), device_id_type=MESH,
            ),
            pltpu.make_async_remote_copy(
                ysend.at[st, 1], yrecv.at[st, 0], hy_send.at[st, 1], hy_recv.at[st, 0],
                device_id=(gx, yup), device_id_type=MESH,
            ),
        )

    def send_halos(st, u):
        for h in range(2):
            for c in range(5):
                for side, first in ((0, 0), (1, 15)):
                    for part in range(2):
                        lo = u[h, c, pl.ds(first + part * 256, 8, stride=16), :]
                        hi = u[h, c, pl.ds(first + part * 256 + 128, 8, stride=16), :]
                        ysend[st, side, h, c, pl.ds(part * 16, 16), :] = jnp.concatenate(
                            [lo, hi], axis=0
                        ).astype(BF16)
        copies = halo_copies(st, u)
        for c in copies:
            c.start()

    def face_copies(st):
        remote = [
            pltpu.make_async_remote_copy(
                fsend.at[st], frecv[st].at[gy], fc_send.at[st, i], fc_recv.at[st, i],
                device_id=(gx, p), device_id_type=MESH,
            )
            for i, p in enumerate(peers)
        ]
        mine = pltpu.make_async_copy(fsend.at[st], frecv[st].at[gy], fc_send.at[st, PEERS - 1])
        return remote, mine

    def send_faces(st, u):
        for s in range(BCAP):
            for c in range(5):
                lo = u[s, c, pl.ds(0, 8, stride=64), :]
                hi = u[s, c, pl.ds(63, 8, stride=64), :]
                fsend[st, s, c] = jnp.concatenate([lo, hi], axis=0).astype(BF16)
        remote, mine = face_copies(st)
        for c in remote:
            c.start()
        mine.start()

    def off_p(u):
        def body(x, _):
            rows = pl.ds(pl.multiple_of(x * 16, 16), 16)
            w = [jnp.concatenate([u[0, c, rows, :], u[1, c, rows, :]], axis=1) for c in range(5)]
            rho, mx, my, mz, en = w
            vx, vy, vz, p, q, h = primitives(w)
            txz, tyz = mx * vz, my * vz
            vals = {
                TXX: mx * vx + p, TXY: mx * vy, TXZ: txz, TYY: my * vy + p, TYZ: tyz,
                HX: h * vx, HY: h * vy, VX: vx, VY: vy, VZ: vz, Q: q, MX: mx, MY: my,
            }
            for k, v in vals.items():
                so[k, 0, x + 1, pl.ds(8, 16), :] = v[:, :128]
                so[k, 1, x + 1, pl.ds(8, 16), :] = v[:, 128:]
            flux = jnp.concatenate([mz, txz, tyz, mz * vz + p, h * vz], axis=0).astype(BF16)
            visc = jnp.concatenate([vx, vy, vz, q], axis=0) * 1.6
            df = jnp.dot(flux, zoff[0], preferred_element_type=F32)
            sf = jnp.dot(visc.astype(BF16), zoff[1], preferred_element_type=F32)
            for c in range(5):
                r = df[16 * c : 16 * c + 16]
                if c:
                    r = r + sf[16 * c - 16 : 16 * c]
                rzo[0, c, rows, :] = r[:, :128]
                rzo[1, c, rows, :] = r[:, 128:]
            return 0

        lax.fori_loop(0, 32, body, 0)

    def off_ghosts(st):
        for side, plane in ((0, 0), (1, 33)):
            for h in range(2):
                w = [xrecv[st, side, h, c] for c in range(5)]
                for k, v in zip(XK, x_terms(w)):
                    so[k, h, plane, pl.ds(8, 16), :] = v
            for h in range(2):
                w = [yrecv[st, side, h, c].astype(F32) for c in range(5)]
                for i, v in enumerate(y_terms(w)):
                    go[i, side, h] = v

    def off_r(u, a, b):
        first = lax.broadcasted_iota(jnp.int32, (8, 128), 0) == 0
        last = lax.broadcasted_iota(jnp.int32, (8, 128), 0) == 7

        def body(x, _):
            for h in range(2):
                for g in range(2):
                    mid = pl.ds(8 + 8 * g, 8)
                    rows = pl.ds(pl.multiple_of(x * 16 + 8 * g, 8), 8)
                    t = (x // 8) * 4 + g * 2 + h
                    ch = jnp.where(tab[S_OFF + t] >= 0, 0.0, DT * b)
                    yl, yh = [], []
                    for i, k in enumerate(YK):
                        l = so[k, h, x + 1, pl.ds(7 + 8 * g, 8), :]
                        r = so[k, h, x + 1, pl.ds(9 + 8 * g, 8), :]
                        if g == 0:
                            e = jnp.broadcast_to(go[i, 0, h, pl.ds(x, 1), :], (8, 128))
                            l = jnp.where(first, e, l)
                        else:
                            e = jnp.broadcast_to(go[i, 1, h, pl.ds(x, 1), :], (8, 128))
                            r = jnp.where(last, e, r)
                        yl.append(l)
                        yh.append(r)
                    for c in range(5):
                        d = so[XF[c], h, x + 2, mid, :] - so[XF[c], h, x, mid, :]
                        d = d + (yh[c] - yl[c])
                        r = rzo[h, c, rows, :] - 0.5 * d
                        if c:
                            k = VF[c - 1]
                            s = so[k, h, x + 2, mid, :] + so[k, h, x, mid, :]
                            s = s + (yh[4 + c] + yl[4 + c])
                            r = r + (0.8 * s - 3.2 * so[k, h, x + 1, mid, :])
                        v = ch * r + (u[h, c, rows, :] if b == 1.0 else b * u[h, c, rows, :])
                        if a:
                            v = v + a * u0o[h, c, rows, :]
                        uo[h, c, rows, :] = v
            return 0

        lax.fori_loop(0, 32, body, 0)

    def near_p(u):
        def body(i, _):
            s = i // 8
            n = lax.rem(i, 8)
            for ch in range(4):
                rows = pl.ds(pl.multiple_of(n * 64 + ch * 16, 16), 16)
                w = [u[s, c, rows, :] for c in range(5)]
                rho, mx, my, mz, en = w
                vx, vy, vz, p, q, h = primitives(w)
                txz, tyz = mx * vz, my * vz
                vals = {
                    TXX: mx * vx + p, TXY: mx * vy, TXZ: txz, TYY: my * vy + p, TYZ: tyz,
                    HX: h * vx, HY: h * vy, VX: vx, VY: vy, VZ: vz, Q: q, MX: mx, MY: my,
                }
                for k, v in vals.items():
                    sn[k, s, n, pl.ds(8 + ch * 16, 16), :] = v
                flux = jnp.concatenate([mz, txz, tyz, mz * vz + p, h * vz], axis=0).astype(BF16)
                visc = jnp.concatenate([vx, vy, vz, q], axis=0).astype(BF16)
                df = jnp.dot(flux, znear[0], preferred_element_type=F32)
                sf = jnp.dot(visc, znear[1], preferred_element_type=F32)
                gz = met[s, 2, rows, :]
                gz2 = 0.8 * gz * gz
                for c in range(5):
                    r = gz * df[16 * c : 16 * c + 16]
                    if c:
                        r = r + gz2 * sf[16 * c - 16 : 16 * c]
                    rzn[s, c, rows, :] = r
            return 0

        lax.fori_loop(0, 8 * BCAP, body, 0)

    def near_ghosts(st):
        for s in range(BCAP):
            for side, base, part in ((0, S_LO, 8), (1, S_HI, 0)):
                at = tab[base + s]
                w = [
                    frecv[st][at // 3, lax.rem(at, 3), c].astype(F32)[part : part + 8]
                    for c in range(5)
                ]
                for i, v in enumerate(y_terms(w)):
                    gn[i, side, s] = v

    def near_r(u, a, b, final):
        first = lax.broadcasted_iota(jnp.int32, (8, 128), 0) == 0
        last = lax.broadcasted_iota(jnp.int32, (8, 128), 0) == 7

        def slot(s):
            keep = tab[S_OCC + s] > 0

            def body(n, _):
                nm = jnp.maximum(n - 1, 0)
                np_ = jnp.minimum(n + 1, 7)
                sign = jnp.where(n == 0, -1.0, 1.0)
                for qd in range(8):
                    mid = pl.ds(8 + 8 * qd, 8)
                    rows = pl.ds(pl.multiple_of(n * 64 + 8 * qd, 8), 8)
                    ch = jnp.where(tab[S_NEAR + s * 8 + qd] >= 0, 0.0, DT * b)
                    gxm, gym = met[s, 0, rows, :], met[s, 1, rows, :]
                    hx, hy = -0.5 * gxm, -0.5 * gym
                    gx2, gy2 = 0.8 * gxm * gxm, 0.8 * gym * gym
                    yl, yh = [], []
                    for i, k in enumerate(YK):
                        l = sn[k, s, n, pl.ds(7 + 8 * qd, 8), :]
                        r = sn[k, s, n, pl.ds(9 + 8 * qd, 8), :]
                        if qd == 0:
                            e = jnp.broadcast_to(gn[i, 0, s, pl.ds(n, 1), :], (8, 128))
                            l = jnp.where(first, e, l)
                        if qd == 7:
                            e = jnp.broadcast_to(gn[i, 1, s, pl.ds(n, 1), :], (8, 128))
                            r = jnp.where(last, e, r)
                        yl.append(l)
                        yh.append(r)
                    for c in range(5):
                        lo = sn[XF[c], s, nm, mid, :]
                        if c in (0, 4):
                            lo = sign * lo
                        r = rzn[s, c, rows, :] + hx * (sn[XF[c], s, np_, mid, :] - lo)
                        r = r + hy * (yh[c] - yl[c])
                        if c:
                            k = VF[c - 1]
                            f2 = sn[k, s, n, mid, :]
                            f2 = f2 + f2
                            lo = sn[k, s, nm, mid, :]
                            if c < 4:
                                lo = sign * lo
                            r = r + gx2 * (sn[k, s, np_, mid, :] + lo - f2)
                            r = r + gy2 * (yh[4 + c] + yl[4 + c] - f2)
                        v = ch * r + (u[s, c, rows, :] if b == 1.0 else b * u[s, c, rows, :])
                        if a:
                            v = v + a * u0n[s, c, rows, :]
                        if final:
                            v = jnp.where(keep, v, 0.0)
                        un[s, c, rows, :] = v
                return 0

            lax.fori_loop(0, 8, body, 0)

        outs = []
        for s in range(BCAP):
            slot(s)
            if final:
                outs.append(pltpu.make_async_copy(un.at[s], near_out.at[s], out_sem.at[2 + s]))
                outs[-1].start()
        return outs

    send_halos(0, u0o)
    send_faces(0, u0n)
    for st in range(3):
        a, b = RK[st]
        uoff = uo if st else u0o
        unear = un if st else u0n
        off_p(uoff)
        near_p(unear)
        for c in halo_copies(st, uoff):
            c.wait_send()
            c.wait_recv()
        off_ghosts(st)
        off_r(uoff, a, b)
        if st < 2:
            send_halos(st + 1, uo)
        else:
            oc = [
                pltpu.make_async_copy(uo.at[h], off_out.at[:, :, pl.ds(128 * h, 128)], out_sem.at[h])
                for h in range(2)
            ]
            for c in oc:
                c.start()
        remote, mine = face_copies(st)
        mine.wait()
        for c in remote:
            c.wait_send()
            c.wait_recv()
        near_ghosts(st)
        outs = near_r(unear, a, b, st == 2)
        if st < 2:
            send_faces(st + 1, un)
    for c in oc + outs:
        c.wait()


def advance(tab, off, near, metric, send, zoff, znear):
    return pl.pallas_call(
        main_kernel,
        out_shape=(
            jax.ShapeDtypeStruct((5, 512, 256), F32),
            jax.ShapeDtypeStruct((BCAP, 5, 512, 128), F32),
        ),
        in_specs=[pl.BlockSpec(memory_space=pltpu.SMEM)]
        + [pl.BlockSpec(memory_space=pl.ANY)] * 4
        + [pl.BlockSpec(memory_space=pltpu.VMEM)] * 2,
        out_specs=(pl.BlockSpec(memory_space=pl.ANY), pl.BlockSpec(memory_space=pl.ANY)),
        scratch_shapes=[
            pltpu.VMEM((2, 5, 512, 128), F32),
            pltpu.VMEM((BCAP, 5, 512, 128), F32),
            pltpu.VMEM((2, 5, 512, 128), F32),
            pltpu.VMEM((BCAP, 5, 512, 128), F32),
            pltpu.VMEM((BCAP, 3, 512, 128), F32),
            pltpu.VMEM((13, 2, 34, 32, 128), F32),
            pltpu.VMEM((13, BCAP, 8, 80, 128), F32),
            pltpu.VMEM((2, 5, 512, 128), F32),
            pltpu.VMEM((BCAP, 5, 512, 128), F32),
            pltpu.VMEM((2, PEERS, 320, 128), BF16),
            pltpu.VMEM((3, BCAP, 5, 16, 128), BF16),
            pltpu.VMEM((PEERS, BCAP, 5, 16, 128), BF16),
            pltpu.VMEM((PEERS, BCAP, 5, 16, 128), BF16),
            pltpu.VMEM((PEERS, BCAP, 5, 16, 128), BF16),
            pltpu.VMEM((3, 2, 2, 5, 16, 128), F32),
            pltpu.VMEM((3, 2, 2, 5, 32, 128), BF16),
            pltpu.VMEM((3, 2, 2, 5, 32, 128), BF16),
            pltpu.VMEM((9, 2, 2, 32, 128), F32),
            pltpu.VMEM((9, 2, BCAP, 8, 128), F32),
            pltpu.SemaphoreType.DMA((4,)),
            pltpu.SemaphoreType.DMA((5,)),
            pltpu.SemaphoreType.DMA((2, PEERS)),
            pltpu.SemaphoreType.DMA((2, PEERS)),
            pltpu.SemaphoreType.DMA((3, PEERS)),
            pltpu.SemaphoreType.DMA((3, PEERS)),
            pltpu.SemaphoreType.DMA((3, 2)),
            pltpu.SemaphoreType.DMA((3, 2)),
            pltpu.SemaphoreType.DMA((3, 2)),
            pltpu.SemaphoreType.DMA((3, 2)),
        ],
        compiler_params=pltpu.CompilerParams(
            collective_id=0, has_side_effects=True, vmem_limit_bytes=67043328
        ),
        name="advance",
    )(tab, off, near, metric, send, zoff, znear)


def z_matrices(width, wrap):
    row = lax.broadcasted_iota(jnp.int32, (width, width), 0)
    col = lax.broadcasted_iota(jnp.int32, (width, width), 1)
    if wrap:
        up, down = (col + 1) % width, (col + width - 1) % width
    else:
        up, down = jnp.minimum(col + 1, width - 1), jnp.maximum(col - 1, 0)
    above = (row == up).astype(F32)
    below = (row == down).astype(F32)
    centre = (row == col).astype(F32)
    scale = 0.5 if wrap else 1.0
    first = -0.5 * (above - below)
    second = scale * (above + below - 2.0 * centre)
    return jnp.stack([first, second]).astype(BF16)


def local(
    off_state,
    near_state,
    near_metric,
    slot_block,
    block_faces,
    fringe_in,
    fringe_in_maps,
    fringe_out,
    fringe_out_maps,
):
    rows = jnp.arange(PEERS, dtype=jnp.int32)

    def labels(table):
        hit = table[1][None, :] == rows[:, None]
        return jnp.sum(jnp.where(hit, table[2][None, :] + 1, 0), axis=1) - 1

    mine = jnp.concatenate(
        [
            labels(fringe_in)[:, None],
            labels(fringe_out)[:, None],
            jnp.broadcast_to(slot_block[None, :], (PEERS, BCAP)),
        ],
        axis=1,
    )
    theirs = lax.all_to_all(mine, "gy", split_axis=0, concat_axis=0, tiled=True)

    def sources(column, count):
        hit = column[None, :] == jnp.arange(count, dtype=jnp.int32)[:, None]
        return jnp.sum(jnp.where(hit, rows[None, :] + 1, 0), axis=1) - 1

    held = theirs[:, 2:].reshape(-1)
    faces = block_faces[jnp.maximum(slot_block, 0)]
    where_at = jnp.arange(PEERS * BCAP, dtype=jnp.int32)

    def position(ids):
        return jnp.sum(jnp.where(held[None, :] == ids[:, None], where_at[None, :], 0), axis=1)

    tab = jnp.concatenate(
        [
            sources(theirs[:, 0], NT_OFF),
            sources(theirs[:, 1], NT_NEAR),
            position(faces[:, 0]),
            position(faces[:, 1]),
            (slot_block >= 0).astype(jnp.int32),
        ]
    ).astype(jnp.int32)
    send = interpolate(
        fringe_in, fringe_out, off_state, near_state, fringe_in_maps, fringe_out_maps
    )
    off_next, near_next = advance(
        tab,
        off_state.reshape(5, 512, 256),
        near_state.reshape(BCAP, 5, 512, 128),
        near_metric.reshape(BCAP, 3, 512, 128),
        send,
        z_matrices(256, True),
        z_matrices(128, False),
    )
    return off_next.reshape(off_state.shape), near_next.reshape(near_state.shape)


def solution(mesh):
    in_specs = (
        P(None, "gx", "gy", None),
        P(("gx", "gy"), None, None, None, None),
        P(("gx", "gy"), None, None, None, None),
        P(("gx", "gy")),
        P(),
        P(None, ("gx", "gy")),
        P(("gx", "gy"), None, None),
        P(None, ("gx", "gy")),
        P(("gx", "gy"), None, None),
    )
    out_specs = (P(None, "gx", "gy", None), P(("gx", "gy"), None, None, None, None))
    return jax.shard_map(local, mesh=mesh, in_specs=in_specs, out_specs=out_specs, check_vma=False)
```

time: 872 us -> 147 us (0.17)
  the two profiles are of different devices: /device:TPU:6 before, /device:TPU:10 now
where the time goes in v1:
time: 147 us
  Pallas kernels  115 us (78%)
  local copies, waits for them, and re-layouts  18.1 us (12%)
  starting transfers between devices  8.41 us (6%)
  other arithmetic  5.04 us (3%)
    pallas_call x1, Pallas kernels, advance(): pl.pallas_call(main_kernel, out_shape=(jax.ShapeDtypeStruct((5, 512, 256)...  110 us
    unnamed x19, local copies, waits for them, and re-layouts  15.1 us
    all_to_all x1, starting transfers between devices, local(): theirs = lax.all_to_all(mine, 'gy', split_axis=0, concat_axis=0, tiled=True)  8.41 us
    pallas_call x1, Pallas kernels, interpolate(): pl.pallas_call(interp_kernel, out_shape=jax.ShapeDtypeStruct((2, PEERS, 3...  4.11 us
  transfers between devices with their start and end apart: 1, of which 0 were waited for; matrix products, arithmetic and copies ran while one was open for 3% of the time, Pallas kernels for 3%

profile of v1, /device:TPU:10, one launch (start us, length us, event | category | flops | bytes accessed | tf_op | source)
XLA Modules:
  0.0 146.9 jit_solution(13284437364048332323)
XLA Ops:
  0.6 0.8 slice_bitcast_fusion.3
  1.4 0.8 slice_bitcast_fusion.2
  2.2 0.7 pad.6.clone
  3.1 0.7 copy.19
  3.8 8.4 %all-to-all-start = ((s32[16,1,5]{2,1,0:T(1,128)}), s32[16,1,5]{2,1,0:T(1,128)S(1)}, u32[]{:S(2)}, u32[]{:S(2)}) async-start(s32[16,1,5]{2,1,0:T(1,128)} %copy.19), calls=%async_computation | async-start | bytes 16384 | tf_op jit(solution)/shard_map/all_to_all | solution.py:602
  12.2 0.7 compare_convert_fusion
  12.9 0.7 broadcast_maximum_fusion
  13.6 0.8 copy.22
  14.4 0.6 gather_fusion
  15.2 0.6 pad_maximum_fusion.1.znear
  15.9 0.7 pad_maximum_fusion.zoff
  16.7 2.1 %copy-done = f32[3,5,8,64,128]{4,3,2,1,0:T(8,128)S(1)} copy-done((f32[3,5,8,64,128]{4,3,2,1,0:T(8,128)S(1)}, f32[3,5,8,64,128]{4,3,2,1,0:T(8,128)}, u32[]{:S(2)}) %copy-start) | copy-done | bytes 3932184
  18.8 1.7 %copy-done.1 = f32[5,32,16,256]{3,2,1,0:T(8,128)S(1)} copy-done((f32[5,32,16,256]{3,2,1,0:T(8,128)S(1)}, f32[5,32,16,256]{3,2,1,0:T(8,128)}, u32[]{:S(2)}) %copy-start.1) | copy-done | bytes 2621464
  20.5 0.9 copy-done.3
  21.5 0.9 copy-done.4
  22.4 0.7 copy-done.5
  23.1 0.7 copy-done.6
  23.8 4.1 %interp.1.send = bf16[2,16,320,128]{3,2,1,0:T(8,128)(2,1)S(1)} custom-call(s32[3,8]{1,0:T(4,128)S(1)} %copy-done.6, s32[3,8]{1,0:T(4,128)S(1)} %copy-done.5, f32[5,32,16,256]{3,2,1,0:T(8,128)S(1)} %copy-done.1, f32[3,5,8,64,128]{4,3,2,1,0:T(8,128)S(1)} %copy-done, bf16[8,128,128]{2,1,0:T(8,128)(2,1)S(1)} %copy-done.3, bf16[8,128,128]{2,1,0:T(8,128)(2,1)S(1)} %copy-done.4), custom_call_target="tpu_custom_call" | custom-call | tf_op jit(solution)/shard_map/interp/pallas_call | solution.py:91
  27.9 1.5 %copy-done.2 = bf16[2,16,320,128]{3,2,1,0:T(8,128)(2,1)} copy-done((bf16[2,16,320,128]{3,2,1,0:T(8,128)(2,1)}, bf16[2,16,320,128]{3,2,1,0:T(8,128)(2,1)S(1)}, u32[]{:S(2)}) %copy-start.2) | copy-done | bytes 2621464
  29.9 0.2 select_reduce_fusion.4
  30.1 0.6 concatenate.7.tab
  30.7 110.5 %advance.1 = (f32[5,512,256]{2,1,0:T(8,128)}, f32[3,5,512,128]{3,2,1,0:T(8,128)}) custom-call(s32[49]{0:T(128)} %concatenate.7.tab, f32[5,512,256]{2,1,0:T(8,128)} %bitcast.25, f32[3,5,512,128]{3,2,1,0:T(8,128)} %bitcast.24, f32[3,3,512,128]{3,2,1,0:T(8,128)} %bitcast.28, bf16[2,16,320,128]{3,2,1,0:T(8,128)(2,1)} %copy-done.2, ...), custom_call_target="tpu_custom_call" | custom-call | tf_op jit(solution)/shard_map/advance/pallas_call | solution.py:513
  141.2 3.8 %copy.25 = f32[5,32,16,256]{3,2,1,0:T(8,128)} copy(f32[5,32,16,256]{3,2,1,0:T(8,128)} %bitcast.27) | data formatting | bytes 5242880
  145.0 1.9 %copy.26 = f32[3,5,8,64,128]{4,3,2,1,0:T(8,128)} copy(f32[3,5,8,64,128]{4,3,2,1,0:T(8,128)S(1)} %bitcast.26) | data formatting | bytes 7864320
  (32 shorter events, 1.1 us)
Async XLA Ops:
  3.8 25.6 %all-to-all-start = ((s32[16,1,5]{2,1,0:T(1,128)}), s32[16,1,5]{2,1,0:T(1,128)S(1)}, u32[]{:S(2)}, u32[]{:S(2)}) async-start(s32[16,1,5]{2,1,0:T(1,128)} %copy.19), calls=%async_computation | async-start | bytes 16384 | tf_op jit(solution)/shard_map/all_to_all | solution.py:602
  16.7 2.1 %copy-start = (f32[3,5,8,64,128]{4,3,2,1,0:T(8,128)S(1)}, f32[3,5,8,64,128]{4,3,2,1,0:T(8,128)}, u32[]{:S(2)}) copy-start(f32[3,5,8,64,128]{4,3,2,1,0:T(8,128)} %near.1) | copy-start | bytes 11796484
  18.8 1.7 %copy-start.1 = (f32[5,32,16,256]{3,2,1,0:T(8,128)S(1)}, f32[5,32,16,256]{3,2,1,0:T(8,128)}, u32[]{:S(2)}) copy-start(f32[5,32,16,256]{3,2,1,0:T(8,128)} %off.1) | copy-start | bytes 7864324
  20.5 0.9 copy-start.3
  21.5 0.9 copy-start.4
  22.4 0.7 copy-start.5
  23.1 0.7 copy-start.6
  27.9 1.5 %copy-start.2 = (bf16[2,16,320,128]{3,2,1,0:T(8,128)(2,1)}, bf16[2,16,320,128]{3,2,1,0:T(8,128)(2,1)S(1)}, u32[]{:S(2)}) copy-start(bf16[2,16,320,128]{3,2,1,0:T(8,128)(2,1)S(1)} %interp.1.send) | copy-start | bytes 7864324
  141.2 3.8 %copy-start.7 = (f32[3,5,512,128]{3,2,1,0:T(8,128)S(1)}, f32[3,5,512,128]{3,2,1,0:T(8,128)}, u32[]{:S(2)}) copy-start(f32[3,5,512,128]{3,2,1,0:T(8,128)} %get-tuple-element.5) | copy-start | bytes 11796484

commit v2 on v1

v2 whole, which is shorter than its diff:
```python
import jax
import jax.numpy as jnp
import numpy as np
from jax import lax
from jax.experimental import pallas as pl
from jax.experimental.pallas import tpu as pltpu
from jax.sharding import PartitionSpec as P

MESH = pl.DeviceIdType.MESH
F32 = jnp.float32
BF16 = jnp.bfloat16

TW = 8
TL = 128
BCAP = 3
NROW = 8
NT_OFF = 16
NT_NEAR = 24
PEERS = 16
DT = 0.1
RK = ((0.0, 1.0), (0.75, 0.25), (1.0 / 3.0, 2.0 / 3.0))

TXX, TXY, TXZ, TYY, TYZ, HX, HY, VX, VY, VZ, Q, MX, MY = range(13)
XF = (MX, TXX, TXY, TXZ, HX)
YF = (MY, TXY, TYY, TYZ, HY)
VF = (VX, VY, VZ, Q)
XK = XF + VF
YK = YF + VF

S_OFF, S_NEAR, S_LO, S_HI, S_OCC = 0, 16, 40, 43, 46


def primitives(u):
    rho, mx, my, mz, en = u
    r = 1.0 / rho
    vx, vy, vz = mx * r, my * r, mz * r
    mv = mx * vx + my * vy + mz * vz
    p = 0.4 * en - 0.2 * mv
    q = r * (0.5 * mv + 1.4 * p)
    return vx, vy, vz, p, q, en + p


def x_terms(u):
    vx, vy, vz, p, q, h = primitives(u)
    mx = u[1]
    return (mx, mx * vx + p, mx * vy, mx * vz, h * vx, vx, vy, vz, q)


def y_terms(u):
    vx, vy, vz, p, q, h = primitives(u)
    my = u[2]
    return (my, my * vx, my * vy + p, my * vz, h * vy, vx, vy, vz, q)


OFFSETS = [((2 + i // 4) % 4, (2 + i % 4) % 4) for i in range(16)]
REMOTE = [i for i in range(16) if OFFSETS[i] != (0, 0)]
SELF = OFFSETS.index((0, 0))


def main_kernel(
    fin,
    fout,
    slot,
    faces,
    off,
    near,
    metric,
    maps_in_hbm,
    maps_out_hbm,
    zoff_hbm,
    znear_hbm,
    off_out,
    near_out,
    u0o,
    u0n,
    uo,
    un,
    met,
    so,
    sn,
    rzo,
    rzn,
    maps_in,
    maps_out,
    zoff,
    znear,
    send_in,
    send_out,
    recv_in,
    recv_out,
    tsend,
    trecv,
    fsend,
    frecv0,
    frecv1,
    frecv2,
    xrecv,
    ysend,
    yrecv,
    go,
    gn,
    ts,
    tab,
    load_sem,
    out_sem,
    t_send,
    t_recv,
    fr_send,
    fr_recv,
    fc_send,
    fc_recv,
    hx_send,
    hx_recv,
    hy_send,
    hy_recv,
):
    frecv = (frecv0, frecv1, frecv2)
    gx = lax.axis_index("gx")
    gy = lax.axis_index("gy")
    nx = 8
    yy, zz = gy // 4, lax.rem(gy, 4)

    def at(dy, dz):
        return lax.rem(yy + dy, 4) * 4 + lax.rem(zz + dz, 4)

    peers = [at(*OFFSETS[i]) for i in REMOTE]
    xup, xdn = lax.rem(gx + 1, nx), lax.rem(gx + nx - 1, nx)
    yup, ydn = lax.rem(gy + 1, PEERS), lax.rem(gy + PEERS - 1, PEERS)

    loads = [
        pltpu.make_async_copy(near, u0n, load_sem.at[0]),
        pltpu.make_async_copy(maps_in_hbm, maps_in, load_sem.at[1]),
        pltpu.make_async_copy(off.at[:, :, pl.ds(0, 128)], u0o.at[0], load_sem.at[2]),
        pltpu.make_async_copy(off.at[:, :, pl.ds(128, 128)], u0o.at[1], load_sem.at[3]),
        pltpu.make_async_copy(maps_out_hbm, maps_out, load_sem.at[4]),
        pltpu.make_async_copy(zoff_hbm, zoff, load_sem.at[5]),
        pltpu.make_async_copy(znear_hbm, znear, load_sem.at[6]),
        pltpu.make_async_copy(metric, met, load_sem.at[7]),
    ]
    for c in loads:
        c.start()

    barrier = pltpu.get_barrier_semaphore()
    for p in peers:
        pl.semaphore_signal(barrier, inc=1, device_id=(gx, p), device_id_type=MESH)
    for p in (xup, xdn):
        pl.semaphore_signal(barrier, inc=1, device_id=(p, gy), device_id_type=MESH)

    lane = lax.broadcasted_iota(jnp.int32, (8, 128), 1)
    table = jnp.full((8, 128), -1, jnp.int32)
    for k in range(NROW):
        table = jnp.where(lane == fin[1, k], fin[2, k], table)
        table = jnp.where(lane == 16 + fout[1, k], fout[2, k], table)
    for s in range(BCAP):
        table = jnp.where(lane == 32 + s, slot[s], table)
    tsend[...] = table

    def interpolate(d, first):
        rows_of, maps, out = ((fin, maps_in, send_in), (fout, maps_out, send_out))[d]

        def body(i, _):
            dest = at(2 + i // 4, 2 + lax.rem(i, 4))
            k = jnp.int32(0)
            for r in range(1, NROW):
                k = jnp.where(rows_of[1, r] == dest, r, k)
            t = rows_of[0, k]
            pieces = []
            for c in range(5):
                for n in range(8):
                    if d == 0:
                        at_row = lax.rem(t, 8) * 8 + n * 64
                        pieces.append(u0n[lax.div(t, 8), c, pl.ds(at_row, 8), :])
                    else:
                        at_row = lax.div(t, 4) * 128 + lax.rem(lax.div(t, 2), 2) * 8 + n * 16
                        pieces.append(u0o[lax.rem(t, 2), c, pl.ds(at_row, 8), :])
            x = jnp.concatenate(pieces, axis=0).astype(BF16)
            out[i] = jnp.dot(x, maps[k], preferred_element_type=F32).astype(BF16)
            return 0

        lax.fori_loop(first, first + 4, body, 0)

    def direct(d, i):
        src = (send_in, send_out)[d].at[i]
        dst = (recv_in, recv_out)[d].at[gy]
        if i == SELF:
            return pltpu.make_async_copy(src, dst, fr_send.at[d, i])
        return pltpu.make_async_remote_copy(
            src, dst, fr_send.at[d, i], fr_recv.at[d, i],
            device_id=(gx, at(*OFFSETS[i])), device_id_type=MESH,
        )

    def start_rows(d, first):
        for i in range(first, first + 4):
            direct(d, i).start()

    def finish_rows(d):
        for i in range(16):
            c = direct(d, i)
            if i == SELF:
                c.wait()
            else:
                c.wait_send()
                c.wait_recv()

    loads[0].wait()
    loads[1].wait()
    interpolate(0, 0)
    pl.semaphore_wait(barrier, PEERS + 1)
    tables = [
        pltpu.make_async_remote_copy(
            tsend, trecv.at[gy], t_send.at[i], t_recv.at[i], device_id=(gx, p), device_id_type=MESH
        )
        for i, p in enumerate(peers)
    ]
    own_table = pltpu.make_async_copy(tsend, trecv.at[gy], t_send.at[PEERS - 1])
    for c in tables:
        c.start()
    own_table.start()
    interpolate(0, 4)
    start_rows(0, 0)
    interpolate(0, 8)
    start_rows(0, 4)
    interpolate(0, 12)
    start_rows(0, 8)
    for c in loads[2:5]:
        c.wait()
    interpolate(1, 0)
    start_rows(0, 12)
    interpolate(1, 4)
    interpolate(1, 8)
    interpolate(1, 12)

    own_table.wait()
    for c in tables:
        c.wait_send()
        c.wait_recv()
    to_scalar = pltpu.make_async_copy(trecv, ts, load_sem.at[8])
    to_scalar.start()
    to_scalar.wait()

    def find_off(t, _):
        src = jnp.int32(-1)
        for g in range(PEERS):
            src = jnp.where(ts[g, 0, gy] == t, g, src)
        tab[S_OFF + t] = src
        return 0

    def find_near(t, _):
        src = jnp.int32(-1)
        for g in range(PEERS):
            src = jnp.where(ts[g, 0, 16 + gy] == t, g, src)
        tab[S_NEAR + t] = src
        return 0

    lax.fori_loop(0, NT_OFF, find_off, 0)
    lax.fori_loop(0, NT_NEAR, find_near, 0)
    for s in range(BCAP):
        tab[S_OCC + s] = jnp.where(slot[s] >= 0, 1, 0)
        block = jnp.maximum(slot[s], 0)
        low, high = faces[0, block], faces[1, block]

        def find_face(g, pos):
            for e in range(BCAP):
                held = ts[g, 0, 32 + e]
                pos = (
                    jnp.where(held == low, g * BCAP + e, pos[0]),
                    jnp.where(held == high, g * BCAP + e, pos[1]),
                )
            return pos

        lo, hi = lax.fori_loop(0, PEERS, find_face, (jnp.int32(0), jnp.int32(0)))
        tab[S_LO + s] = lo
        tab[S_HI + s] = hi

    for c in loads[5:]:
        c.wait()
    finish_rows(0)

    def settle_off(t, _):
        src = tab[S_OFF + t]
        take = src >= 0
        row = jnp.maximum(src, 0)
        half = lax.rem(t, 2)
        base = (t // 4) * 128 + lax.rem(t // 2, 2) * 8
        for c in range(5):
            for a in range(4):
                v = recv_in[row, pl.ds(c * 64 + a * 16, 16), :].astype(F32)
                for b in range(2):
                    rows = pl.ds(pl.multiple_of(base + (2 * a + b) * 16, 8), 8)
                    old = u0o[half, c, rows, :]
                    u0o[half, c, rows, :] = jnp.where(take, v[8 * b : 8 * b + 8], old)
        return 0

    def settle_near(t, _):
        src = tab[S_NEAR + t]
        take = src >= 0
        row = jnp.maximum(src, 0)
        s = t // 8
        base = lax.rem(t, 8) * 8
        for c in range(5):
            for a in range(4):
                v = recv_out[row, pl.ds(c * 64 + a * 16, 16), :].astype(F32)
                for b in range(2):
                    rows = pl.ds(pl.multiple_of(base + (2 * a + b) * 64, 8), 8)
                    old = u0n[s, c, rows, :]
                    u0n[s, c, rows, :] = jnp.where(take, v[8 * b : 8 * b + 8], old)
        return 0


    def halo_copies(st, u):
        return (
            pltpu.make_async_remote_copy(
                u.at[:, :, pl.ds(0, 16), :], xrecv.at[st, 1], hx_send.at[st, 0], hx_recv.at[st, 1],
                device_id=(xdn, gy), device_id_type=MESH,
            ),
            pltpu.make_async_remote_copy(
                u.at[:, :, pl.ds(496, 16), :], xrecv.at[st, 0], hx_send.at[st, 1], hx_recv.at[st, 0],
                device_id=(xup, gy), device_id_type=MESH,
            ),
            pltpu.make_async_remote_copy(
                ysend.at[st, 0], yrecv.at[st, 1], hy_send.at[st, 0], hy_recv.at[st, 1],
                device_id=(gx, ydn), device_id_type=MESH,
            ),
            pltpu.make_async_remote_copy(
                ysend.at[st, 1], yrecv.at[st, 0], hy_send.at[st, 1], hy_recv.at[st, 0],
                device_id=(gx, yup), device_id_type=MESH,
            ),
        )

    def send_halos(st, u):
        for h in range(2):
            for c in range(5):
                for side, first in ((0, 0), (1, 15)):
                    for part in range(2):
                        lo = u[h, c, pl.ds(first + part * 256, 8, stride=16), :]
                        hi = u[h, c, pl.ds(first + part * 256 + 128, 8, stride=16), :]
                        ysend[st, side, h, c, pl.ds(part * 16, 16), :] = jnp.concatenate(
                            [lo, hi], axis=0
                        ).astype(BF16)
        copies = halo_copies(st, u)
        for c in copies:
            c.start()

    def face_copies(st):
        remote = [
            pltpu.make_async_remote_copy(
                fsend.at[st], frecv[st].at[gy], fc_send.at[st, i], fc_recv.at[st, i],
                device_id=(gx, p), device_id_type=MESH,
            )
            for i, p in enumerate(peers)
        ]
        mine = pltpu.make_async_copy(fsend.at[st], frecv[st].at[gy], fc_send.at[st, PEERS - 1])
        return remote, mine

    def send_faces(st, u):
        for s in range(BCAP):
            for c in range(5):
                lo = u[s, c, pl.ds(0, 8, stride=64), :]
                hi = u[s, c, pl.ds(63, 8, stride=64), :]
                fsend[st, s, c] = jnp.concatenate([lo, hi], axis=0).astype(BF16)
        remote, mine = face_copies(st)
        for c in remote:
            c.start()
        mine.start()

    def off_p(u):
        def body(x, _):
            rows = pl.ds(pl.multiple_of(x * 32, 32), 32)
            w = [jnp.concatenate([u[0, c, rows, :], u[1, c, rows, :]], axis=1) for c in range(5)]
            rho, mx, my, mz, en = w
            vx, vy, vz, p, q, h = primitives(w)
            txz, tyz = mx * vz, my * vz
            vals = {
                TXX: mx * vx + p, TXY: mx * vy, TXZ: txz, TYY: my * vy + p, TYZ: tyz,
                HX: h * vx, HY: h * vy, VX: vx, VY: vy, VZ: vz, Q: q, MX: mx, MY: my,
            }
            for k, v in vals.items():
                for e in range(2):
                    so[k, 0, 2 * x + 1 + e, pl.ds(8, 16), :] = v[16 * e : 16 * e + 16, :128]
                    so[k, 1, 2 * x + 1 + e, pl.ds(8, 16), :] = v[16 * e : 16 * e + 16, 128:]
            flux = jnp.concatenate([mz, txz, tyz, mz * vz + p, h * vz], axis=0).astype(BF16)
            visc = jnp.concatenate([vx, vy, vz, q], axis=0) * 1.6
            df = jnp.dot(flux, zoff[0], preferred_element_type=F32)
            sf = jnp.dot(visc.astype(BF16), zoff[1], preferred_element_type=F32)
            for c in range(5):
                r = df[32 * c : 32 * c + 32]
                if c:
                    r = r + sf[32 * c - 32 : 32 * c]
                rzo[0, c, rows, :] = r[:, :128]
                rzo[1, c, rows, :] = r[:, 128:]
            return 0

        lax.fori_loop(0, 16, body, 0, unroll=2)

    def off_ghosts(st):
        for side, plane in ((0, 0), (1, 33)):
            for h in range(2):
                w = [xrecv[st, side, h, c] for c in range(5)]
                for k, v in zip(XK, x_terms(w)):
                    so[k, h, plane, pl.ds(8, 16), :] = v
            for h in range(2):
                w = [yrecv[st, side, h, c].astype(F32) for c in range(5)]
                for i, v in enumerate(y_terms(w)):
                    go[i, side, h] = v

    def off_r(u, a, b):
        first = lax.broadcasted_iota(jnp.int32, (8, 128), 0) == 0
        last = lax.broadcasted_iota(jnp.int32, (8, 128), 0) == 7

        def body(x, _):
            for h in range(2):
                for g in range(2):
                    mid = pl.ds(8 + 8 * g, 8)
                    rows = pl.ds(pl.multiple_of(x * 16 + 8 * g, 8), 8)
                    t = (x // 8) * 4 + g * 2 + h
                    ch = jnp.where(tab[S_OFF + t] >= 0, 0.0, DT * b)
                    yl, yh = [], []
                    for i, k in enumerate(YK):
                        l = so[k, h, x + 1, pl.ds(7 + 8 * g, 8), :]
                        r = so[k, h, x + 1, pl.ds(9 + 8 * g, 8), :]
                        if g == 0:
                            e = jnp.broadcast_to(go[i, 0, h, pl.ds(x, 1), :], (8, 128))
                            l = jnp.where(first, e, l)
                        else:
                            e = jnp.broadcast_to(go[i, 1, h, pl.ds(x, 1), :], (8, 128))
                            r = jnp.where(last, e, r)
                        yl.append(l)
                        yh.append(r)
                    for c in range(5):
                        d = so[XF[c], h, x + 2, mid, :] - so[XF[c], h, x, mid, :]
                        d = d + (yh[c] - yl[c])
                        r = rzo[h, c, rows, :] - 0.5 * d
                        if c:
                            k = VF[c - 1]
                            s = so[k, h, x + 2, mid, :] + so[k, h, x, mid, :]
                            s = s + (yh[4 + c] + yl[4 + c])
                            r = r + (0.8 * s - 3.2 * so[k, h, x + 1, mid, :])
                        v = ch * r + (u[h, c, rows, :] if b == 1.0 else b * u[h, c, rows, :])
                        if a:
                            v = v + a * u0o[h, c, rows, :]
                        uo[h, c, rows, :] = v
            return 0

        lax.fori_loop(0, 32, body, 0, unroll=2)

    def near_p(u):
        def body(i, _):
            s = i // 8
            n = lax.rem(i, 8)
            for ch in range(2):
                rows = pl.ds(pl.multiple_of(n * 64 + ch * 32, 32), 32)
                w = [u[s, c, rows, :] for c in range(5)]
                rho, mx, my, mz, en = w
                vx, vy, vz, p, q, h = primitives(w)
                txz, tyz = mx * vz, my * vz
                vals = {
                    TXX: mx * vx + p, TXY: mx * vy, TXZ: txz, TYY: my * vy + p, TYZ: tyz,
                    HX: h * vx, HY: h * vy, VX: vx, VY: vy, VZ: vz, Q: q, MX: mx, MY: my,
                }
                for k, v in vals.items():
                    sn[k, s, n, pl.ds(8 + ch * 32, 32), :] = v
                flux = jnp.concatenate([mz, txz, tyz, mz * vz + p, h * vz], axis=0).astype(BF16)
                visc = jnp.concatenate([vx, vy, vz, q], axis=0).astype(BF16)
                df = jnp.dot(flux, znear[0], preferred_element_type=F32)
                sf = jnp.dot(visc, znear[1], preferred_element_type=F32)
                gz = met[s, 2, rows, :]
                gz2 = 0.8 * gz * gz
                for c in range(5):
                    r = gz * df[32 * c : 32 * c + 32]
                    if c:
                        r = r + gz2 * sf[32 * c - 32 : 32 * c]
                    rzn[s, c, rows, :] = r
            return 0

        lax.fori_loop(0, 8 * BCAP, body, 0, unroll=2)

    def near_ghosts(st):
        for s in range(BCAP):
            for side, base, part in ((0, S_LO, 8), (1, S_HI, 0)):
                e = tab[base + s]
                w = [
                    frecv[st][lax.div(e, 3), lax.rem(e, 3), c].astype(F32)[part : part + 8]
                    for c in range(5)
                ]
                for i, v in enumerate(y_terms(w)):
                    gn[i, side, s] = v

    def near_r(st, u, a, b, final):
        first = lax.broadcasted_iota(jnp.int32, (8, 128), 0) == 0
        last = lax.broadcasted_iota(jnp.int32, (8, 128), 0) == 7

        def cells(s, n, groups, keep):
            nm = jnp.maximum(n - 1, 0)
            np_ = jnp.minimum(n + 1, 7)
            sign = jnp.where(n == 0, -1.0, 1.0)
            for qd in groups:
                mid = pl.ds(8 + 8 * qd, 8)
                rows = pl.ds(pl.multiple_of(n * 64 + 8 * qd, 8), 8)
                ch = jnp.where(tab[S_NEAR + s * 8 + qd] >= 0, 0.0, DT * b)
                gxm, gym = met[s, 0, rows, :], met[s, 1, rows, :]
                hx, hy = -0.5 * gxm, -0.5 * gym
                gx2, gy2 = 0.8 * gxm * gxm, 0.8 * gym * gym
                yl, yh = [], []
                for i, k in enumerate(YK):
                    l = sn[k, s, n, pl.ds(7 + 8 * qd, 8), :]
                    r = sn[k, s, n, pl.ds(9 + 8 * qd, 8), :]
                    if qd == 0:
                        e = jnp.broadcast_to(gn[i, 0, s, pl.ds(n, 1), :], (8, 128))
                        l = jnp.where(first, e, l)
                    if qd == 7:
                        e = jnp.broadcast_to(gn[i, 1, s, pl.ds(n, 1), :], (8, 128))
                        r = jnp.where(last, e, r)
                    yl.append(l)
                    yh.append(r)
                for c in range(5):
                    lo = sn[XF[c], s, nm, mid, :]
                    if c in (0, 4):
                        lo = sign * lo
                    r = rzn[s, c, rows, :] + hx * (sn[XF[c], s, np_, mid, :] - lo)
                    r = r + hy * (yh[c] - yl[c])
                    if c:
                        k = VF[c - 1]
                        f2 = sn[k, s, n, mid, :]
                        f2 = f2 + f2
                        lo = sn[k, s, nm, mid, :]
                        if c < 4:
                            lo = sign * lo
                        r = r + gx2 * (sn[k, s, np_, mid, :] + lo - f2)
                        r = r + gy2 * (yh[4 + c] + yl[4 + c] - f2)
                    v = ch * r + (u[s, c, rows, :] if b == 1.0 else b * u[s, c, rows, :])
                    if a:
                        v = v + a * u0n[s, c, rows, :]
                    if final:
                        v = jnp.where(keep, v, 0.0)
                    un[s, c, rows, :] = v

        def edges(n, _):
            for s in range(BCAP):
                cells(s, n, (0, 7), tab[S_OCC + s] > 0)
            return 0

        def middle(s):
            keep = tab[S_OCC + s] > 0

            def body(n, _):
                cells(s, n, range(1, 7), keep)
                return 0

            lax.fori_loop(0, 8, body, 0)

        lax.fori_loop(0, 8, edges, 0)
        if not final:
            send_faces(st + 1, un)
        outs = []
        for s in range(BCAP):
            middle(s)
            if final:
                outs.append(pltpu.make_async_copy(un.at[s], near_out.at[s], out_sem.at[2 + s]))
                outs[-1].start()
        return outs

    def off_section(st):
        u = uo if st else u0o
        for c in halo_copies(st, u):
            c.wait_send()
            c.wait_recv()
        off_ghosts(st)
        off_r(u, *RK[st])
        if st < 2:
            send_halos(st + 1, uo)

    def near_section(st):
        remote, mine = face_copies(st)
        mine.wait()
        for c in remote:
            c.wait_send()
            c.wait_recv()
        near_ghosts(st)
        return near_r(st, un if st else u0n, *RK[st], st == 2)

    lax.fori_loop(0, NT_OFF, settle_off, 0)
    send_halos(0, u0o)
    for q in range(4):
        start_rows(1, 4 * q)
    off_p(u0o)
    off_section(0)
    off_p(uo)
    finish_rows(1)
    lax.fori_loop(0, NT_NEAR, settle_near, 0)
    send_faces(0, u0n)
    near_p(u0n)
    off_section(1)
    near_section(0)
    near_p(un)
    off_p(uo)
    near_section(1)
    near_p(un)
    off_section(2)
    oc = [
        pltpu.make_async_copy(uo.at[h], off_out.at[:, :, pl.ds(128 * h, 128)], out_sem.at[h])
        for h in range(2)
    ]
    for c in oc:
        c.start()
    outs = near_section(2)
    for c in oc + outs:
        c.wait()


def advance(fin, fout, slot, faces, off, near, metric, maps_in, maps_out, zoff, znear):
    dma = pltpu.SemaphoreType.DMA
    return pl.pallas_call(
        main_kernel,
        out_shape=(
            jax.ShapeDtypeStruct((5, 512, 256), F32),
            jax.ShapeDtypeStruct((BCAP, 5, 512, 128), F32),
        ),
        in_specs=[pl.BlockSpec(memory_space=pltpu.SMEM)] * 4
        + [pl.BlockSpec(memory_space=pl.ANY)] * 7,
        out_specs=(pl.BlockSpec(memory_space=pl.ANY), pl.BlockSpec(memory_space=pl.ANY)),
        scratch_shapes=[
            pltpu.VMEM((2, 5, 512, 128), F32),
            pltpu.VMEM((BCAP, 5, 512, 128), F32),
            pltpu.VMEM((2, 5, 512, 128), F32),
            pltpu.VMEM((BCAP, 5, 512, 128), F32),
            pltpu.VMEM((BCAP, 3, 512, 128), F32),
            pltpu.VMEM((13, 2, 34, 32, 128), F32),
            pltpu.VMEM((13, BCAP, 8, 80, 128), F32),
            pltpu.VMEM((2, 5, 512, 128), F32),
            pltpu.VMEM((BCAP, 5, 512, 128), F32),
            pltpu.VMEM((NROW, 128, 128), BF16),
            pltpu.VMEM((NROW, 128, 128), BF16),
            pltpu.VMEM((2, 256, 256), BF16),
            pltpu.VMEM((2, 128, 128), BF16),
            pltpu.VMEM((PEERS, 320, 128), BF16),
            pltpu.VMEM((PEERS, 320, 128), BF16),
            pltpu.VMEM((PEERS, 320, 128), BF16),
            pltpu.VMEM((PEERS, 320, 128), BF16),
            pltpu.VMEM((8, 128), jnp.int32),
            pltpu.VMEM((PEERS, 8, 128), jnp.int32),
            pltpu.VMEM((3, BCAP, 5, 16, 128), BF16),
            pltpu.VMEM((PEERS, BCAP, 5, 16, 128), BF16),
            pltpu.VMEM((PEERS, BCAP, 5, 16, 128), BF16),
            pltpu.VMEM((PEERS, BCAP, 5, 16, 128), BF16),
            pltpu.VMEM((3, 2, 2, 5, 16, 128), F32),
            pltpu.VMEM((3, 2, 2, 5, 32, 128), BF16),
            pltpu.VMEM((3, 2, 2, 5, 32, 128), BF16),
            pltpu.VMEM((9, 2, 2, 32, 128), F32),
            pltpu.VMEM((9, 2, BCAP, 8, 128), F32),
            pltpu.SMEM((PEERS, 8, 128), jnp.int32),
            pltpu.SMEM((64,), jnp.int32),
            dma((9,)),
            dma((5,)),
            dma((PEERS,)),
            dma((PEERS,)),
            dma((2, PEERS)),
            dma((2, PEERS)),
            dma((3, PEERS)),
            dma((3, PEERS)),
            dma((3, 2)),
            dma((3, 2)),
            dma((3, 2)),
            dma((3, 2)),
        ],
        compiler_params=pltpu.CompilerParams(
            collective_id=0, has_side_effects=True, vmem_limit_bytes=67043328
        ),
        name="advance",
    )(fin, fout, slot, faces, off, near, metric, maps_in, maps_out, zoff, znear)


def z_matrices(width, wrap):
    col = np.arange(width)
    up, down = np.roll(col, -1), np.roll(col, 1)
    if not wrap:
        up[-1], down[0] = width - 1, 0
    first, second = np.zeros((2, width, width), np.float32)
    scale = 0.5 if wrap else 1.0
    for c in range(width):
        first[up[c], c] -= 0.5
        first[down[c], c] += 0.5
        second[up[c], c] += scale
        second[down[c], c] += scale
        second[c, c] -= 2.0 * scale
    return jnp.asarray(np.stack([first, second]), BF16)


def local(
    off_state,
    near_state,
    near_metric,
    slot_block,
    block_faces,
    fringe_in,
    fringe_in_maps,
    fringe_out,
    fringe_out_maps,
):
    off_next, near_next = advance(
        fringe_in,
        fringe_out,
        slot_block,
        block_faces.T,
        off_state.reshape(5, 512, 256),
        near_state.reshape(BCAP, 5, 512, 128),
        near_metric.reshape(BCAP, 3, 512, 128),
        fringe_in_maps,
        fringe_out_maps,
        z_matrices(256, True),
        z_matrices(128, False),
    )
    return off_next.reshape(off_state.shape), near_next.reshape(near_state.shape)


def solution(mesh):
    in_specs = (
        P(None, "gx", "gy", None),
        P(("gx", "gy"), None, None, None, None),
        P(("gx", "gy"), None, None, None, None),
        P(("gx", "gy")),
        P(),
        P(None, ("gx", "gy")),
        P(("gx", "gy"), None, None),
        P(None, ("gx", "gy")),
        P(("gx", "gy"), None, None),
    )
    out_specs = (P(None, "gx", "gy", None), P(("gx", "gy"), None, None, None, None))
    return jax.shard_map(local, mesh=mesh, in_specs=in_specs, out_specs=out_specs, check_vma=False)
```

time: 147 us -> 105 us (0.71)
  the two profiles are of different devices: /device:TPU:10 before, /device:TPU:6 now
where the time goes in v2:
time: 105 us; the launch traced here: 104 us
  Pallas kernels  97.8 us (93%)
  local copies, waits for them, and re-layouts  5.7 us (5%)
    pallas_call x1, Pallas kernels, advance(): pl.pallas_call(main_kernel, out_shape=(jax.ShapeDtypeStruct((5, 512, 256)...  97.8 us
    unnamed x4, local copies, waits for them, and re-layouts  5.7 us

profile of v2, /device:TPU:6, one launch (start us, length us, event | category | flops | bytes accessed | tf_op | source)
XLA Modules:
  0.0 104.1 jit_solution(824658508896126827)
XLA Ops:
  0.6 97.8 %advance.1 = (f32[5,512,256]{2,1,0:T(8,128)}, f32[3,5,512,128]{3,2,1,0:T(8,128)}) custom-call(s32[3,8]{1,0:T(4,128)} %fin.1, s32[3,8]{1,0:T(4,128)} %fout.1, s32[3]{0:T(128)} %slot.1, s32[2,256]{1,0:T(2,128)} %bitcast.11, f32[5,512,256]{2,1,0:T(8,128)} %bitcast.8, f32[3,5,512,128]{3,2,1,0:T(8,128)} %bitcast.6, f32[3,3,512,128]{3,2,1,0:T(8,128)} %bitcast.10, ...), custom_call_target="tpu_custom_call" | custom-call | tf_op jit(solution)/shard_map/advance/pallas_call | solution.py:612
  98.4 0.0 copy-start
  98.4 3.8 %copy.15 = f32[5,32,16,256]{3,2,1,0:T(8,128)} copy(f32[5,32,16,256]{3,2,1,0:T(8,128)} %bitcast.9) | data formatting | bytes 5242880
  102.2 0.0 copy-done
  102.2 1.9 %copy.16 = f32[3,5,8,64,128]{4,3,2,1,0:T(8,128)} copy(f32[3,5,8,64,128]{4,3,2,1,0:T(8,128)S(1)} %bitcast.7) | data formatting | bytes 7864320
Async XLA Ops:
  98.4 3.8 %copy-start = (f32[3,5,512,128]{3,2,1,0:T(8,128)S(1)}, f32[3,5,512,128]{3,2,1,0:T(8,128)}, u32[]{:S(2)}) copy-start(f32[3,5,512,128]{3,2,1,0:T(8,128)} %get-tuple-element.5) | copy-start | bytes 11796484

commit v3 on v2

--- a/solution.py
+++ b/solution.py
@@ -27,7 +27,7 @@
 XK = XF + VF
 YK = YF + VF
 
-S_OFF, S_NEAR, S_LO, S_HI, S_OCC = 0, 16, 40, 43, 46
+S_OFF, S_NEAR, S_LO, S_HI, S_OCC, S_PICK = 0, 16, 40, 43, 46, 49
 
 
 def primitives(u):
@@ -91,9 +91,13 @@
     tsend,
     trecv,
     fsend,
-    frecv0,
-    frecv1,
-    frecv2,
+    frow0,
+    frow1,
+    frow2,
+    psend,
+    precv0,
+    precv1,
+    precv2,
     xrecv,
     ysend,
     yrecv,
@@ -107,14 +111,17 @@
     t_recv,
     fr_send,
     fr_recv,
-    fc_send,
-    fc_recv,
+    ra_send,
+    ra_recv,
+    rb_send,
+    rb_recv,
     hx_send,
     hx_recv,
     hy_send,
     hy_recv,
 ):
-    frecv = (frecv0, frecv1, frecv2)
+    frow = (frow0, frow1, frow2)
+    precv = (precv0, precv1, precv2)
     gx = lax.axis_index("gx")
     gy = lax.axis_index("gy")
     nx = 8
@@ -125,6 +132,16 @@
 
     peers = [at(*OFFSETS[i]) for i in REMOTE]
     xup, xdn = lax.rem(gx + 1, nx), lax.rem(gx + nx - 1, nx)
+    core = lax.rem(gx, 2)
+    ca = core * yy + (1 - core) * zz
+    cb = core * zz + (1 - core) * yy
+
+    def on_a(d):
+        return at(core * d, (1 - core) * d)
+
+    def on_b(d):
+        return at((1 - core) * d, core * d)
+
     yup, ydn = lax.rem(gy + 1, PEERS), lax.rem(gy + PEERS - 1, PEERS)
 
     loads = [
@@ -269,8 +286,27 @@
             return pos
 
         lo, hi = lax.fori_loop(0, PEERS, find_face, (jnp.int32(0), jnp.int32(0)))
-        tab[S_LO + s] = lo
-        tab[S_HI + s] = hi
+        for base, pos in ((S_LO, lo), (S_HI, hi)):
+            g = lax.div(pos, BCAP)
+            tab[base + s] = jnp.where(core == 0, lax.div(g, 4), lax.rem(g, 4))
+
+    def find_picks(d, _):
+        dest = on_b(d)
+        for s in range(BCAP):
+            block = jnp.maximum(ts[dest, 0, 32 + s], 0)
+            low, high = faces[0, block], faces[1, block]
+            lo, hi = jnp.int32(0), jnp.int32(0)
+            for a in range(4):
+                g = core * (a * 4 + zz) + (1 - core) * (yy * 4 + a)
+                for e in range(BCAP):
+                    held = ts[g, 0, 32 + e]
+                    lo = jnp.where(held == low, a * BCAP + e, lo)
+                    hi = jnp.where(held == high, a * BCAP + e, hi)
+            tab[S_PICK + 6 * d + 2 * s] = lo
+            tab[S_PICK + 6 * d + 2 * s + 1] = hi
+        return 0
+
+    lax.fori_loop(0, 4, find_picks, 0)
 
     for c in loads[5:]:
         c.wait()
@@ -341,27 +377,52 @@
         for c in copies:
             c.start()
 
-    def face_copies(st):
-        remote = [
-            pltpu.make_async_remote_copy(
-                fsend.at[st], frecv[st].at[gy], fc_send.at[st, i], fc_recv.at[st, i],
-                device_id=(gx, p), device_id_type=MESH,
-            )
-            for i, p in enumerate(peers)
-        ]
-        mine = pltpu.make_async_copy(fsend.at[st], frecv[st].at[gy], fc_send.at[st, PEERS - 1])
-        return remote, mine
+    def row_copy(st, d):
+        return pltpu.make_async_remote_copy(
+            fsend.at[st], frow[st].at[ca], ra_send.at[st, d], ra_recv.at[st, d],
+            device_id=(gx, on_a(d)), device_id_type=MESH,
+        )
+
+    def parcel_copy(st, d):
+        return pltpu.make_async_remote_copy(
+            psend.at[st, d], precv[st].at[cb], rb_send.at[st, d], rb_recv.at[st, d],
+            device_id=(gx, on_b(d)), device_id_type=MESH,
+        )
 
     def send_faces(st, u):
         for s in range(BCAP):
             for c in range(5):
                 lo = u[s, c, pl.ds(0, 8, stride=64), :]
                 hi = u[s, c, pl.ds(63, 8, stride=64), :]
-                fsend[st, s, c] = jnp.concatenate([lo, hi], axis=0).astype(BF16)
-        remote, mine = face_copies(st)
-        for c in remote:
-            c.start()
-        mine.start()
+                both = jnp.concatenate([lo, hi], axis=0).astype(BF16)
+                fsend[st, s, c] = both
+                frow[st][ca, s, c] = both
+        for d in (2, 1, 3):
+            row_copy(st, d).start()
+
+    def send_parcels(st):
+        for d in (1, 2, 3):
+            row_copy(st, d).wait_recv()
+        for d in (2, 1, 3, 0):
+            for s in range(BCAP):
+                lo = tab[S_PICK + 6 * d + 2 * s]
+                hi = tab[S_PICK + 6 * d + 2 * s + 1]
+                for c in range(5):
+                    low = frow[st][lax.div(lo, 3), lax.rem(lo, 3), c].astype(F32)[8:]
+                    high = frow[st][lax.div(hi, 3), lax.rem(hi, 3), c].astype(F32)[:8]
+                    both = jnp.concatenate([low, high], axis=0).astype(BF16)
+                    if d:
+                        psend[st, d, s, c] = both
+                    else:
+                        precv[st][cb, s, c] = both
+        for d in (2, 1, 3):
+            parcel_copy(st, d).start()
+
+    def finish_faces(st):
+        for d in (1, 2, 3):
+            row_copy(st, d).wait_send()
+            parcel_copy(st, d).wait_send()
+            parcel_copy(st, d).wait_recv()
 
     def off_p(u):
         def body(x, _):
@@ -476,11 +537,10 @@
 
     def near_ghosts(st):
         for s in range(BCAP):
-            for side, base, part in ((0, S_LO, 8), (1, S_HI, 0)):
-                e = tab[base + s]
+            for side, base in ((0, S_LO), (1, S_HI)):
+                row = tab[base + s]
                 w = [
-                    frecv[st][lax.div(e, 3), lax.rem(e, 3), c].astype(F32)[part : part + 8]
-                    for c in range(5)
+                    precv[st][row, s, c].astype(F32)[8 * side : 8 * side + 8] for c in range(5)
                 ]
                 for i, v in enumerate(y_terms(w)):
                     gn[i, side, s] = v
@@ -554,6 +614,8 @@
         outs = []
         for s in range(BCAP):
             middle(s)
+            if s == 1 and not final:
+                send_parcels(st + 1)
             if final:
                 outs.append(pltpu.make_async_copy(un.at[s], near_out.at[s], out_sem.at[2 + s]))
                 outs[-1].start()
@@ -570,31 +632,26 @@
             send_halos(st + 1, uo)
 
     def near_section(st):
-        remote, mine = face_copies(st)
-        mine.wait()
-        for c in remote:
-            c.wait_send()
-            c.wait_recv()
+        finish_faces(st)
         near_ghosts(st)
         return near_r(st, un if st else u0n, *RK[st], st == 2)
 
     lax.fori_loop(0, NT_OFF, settle_off, 0)
     send_halos(0, u0o)
-    for q in range(4):
-        start_rows(1, 4 * q)
+    start_rows(1, 0)
+    start_rows(1, 4)
     off_p(u0o)
     off_section(0)
+    start_rows(1, 8)
+    start_rows(1, 12)
+    off_p(uo)
+    off_section(1)
     off_p(uo)
     finish_rows(1)
     lax.fori_loop(0, NT_NEAR, settle_near, 0)
     send_faces(0, u0n)
     near_p(u0n)
-    off_section(1)
-    near_section(0)
-    near_p(un)
-    off_p(uo)
-    near_section(1)
-    near_p(un)
+    send_parcels(0)
     off_section(2)
     oc = [
         pltpu.make_async_copy(uo.at[h], off_out.at[:, :, pl.ds(128 * h, 128)], out_sem.at[h])
@@ -602,6 +659,10 @@
     ]
     for c in oc:
         c.start()
+    near_section(0)
+    near_p(un)
+    near_section(1)
+    near_p(un)
     outs = near_section(2)
     for c in oc + outs:
         c.wait()
@@ -639,24 +700,30 @@
             pltpu.VMEM((8, 128), jnp.int32),
             pltpu.VMEM((PEERS, 8, 128), jnp.int32),
             pltpu.VMEM((3, BCAP, 5, 16, 128), BF16),
-            pltpu.VMEM((PEERS, BCAP, 5, 16, 128), BF16),
-            pltpu.VMEM((PEERS, BCAP, 5, 16, 128), BF16),
-            pltpu.VMEM((PEERS, BCAP, 5, 16, 128), BF16),
+            pltpu.VMEM((4, BCAP, 5, 16, 128), BF16),
+            pltpu.VMEM((4, BCAP, 5, 16, 128), BF16),
+            pltpu.VMEM((4, BCAP, 5, 16, 128), BF16),
+            pltpu.VMEM((3, 4, BCAP, 5, 16, 128), BF16),
+            pltpu.VMEM((4, BCAP, 5, 16, 128), BF16),
+            pltpu.VMEM((4, BCAP, 5, 16, 128), BF16),
+            pltpu.VMEM((4, BCAP, 5, 16, 128), BF16),
             pltpu.VMEM((3, 2, 2, 5, 16, 128), F32),
             pltpu.VMEM((3, 2, 2, 5, 32, 128), BF16),
             pltpu.VMEM((3, 2, 2, 5, 32, 128), BF16),
             pltpu.VMEM((9, 2, 2, 32, 128), F32),
             pltpu.VMEM((9, 2, BCAP, 8, 128), F32),
             pltpu.SMEM((PEERS, 8, 128), jnp.int32),
-            pltpu.SMEM((64,), jnp.int32),
+            pltpu.SMEM((80,), jnp.int32),
             dma((9,)),
             dma((5,)),
             dma((PEERS,)),
             dma((PEERS,)),
             dma((2, PEERS)),
             dma((2, PEERS)),
-            dma((3, PEERS)),
-            dma((3, PEERS)),
+            dma((3, 4)),
+            dma((3, 4)),
+            dma((3, 4)),
+            dma((3, 4)),
             dma((3, 2)),
             dma((3, 2)),
             dma((3, 2)),

time: 105 us -> 99 us (0.943)
  Pallas kernels: 97.8 us -> 92.5 us
    pallas_call x1, Pallas kernels: 97.8 us -> 92.5 us  [advance(): pl.pallas_call(main_kernel, out_shape=(jax.ShapeDtypeStruct((5, 512, 256)...]
where the time goes in v3:
time: 99 us; the launch traced here: 98.9 us
  Pallas kernels  92.5 us (93%)
  local copies, waits for them, and re-layouts  5.7 us (6%)
    pallas_call x1, Pallas kernels, advance(): pl.pallas_call(main_kernel, out_shape=(jax.ShapeDtypeStruct((5, 512, 256)...  92.5 us
    unnamed x4, local copies, waits for them, and re-layouts  5.7 us

profile of v3, /device:TPU:6, one launch (start us, length us, event | category | flops | bytes accessed | tf_op | source)
XLA Modules:
  0.0 98.9 jit_solution(1877474773981742771)
XLA Ops:
  0.6 92.5 %advance.1 = (f32[5,512,256]{2,1,0:T(8,128)}, f32[3,5,512,128]{3,2,1,0:T(8,128)}) custom-call(s32[3,8]{1,0:T(4,128)} %fin.1, s32[3,8]{1,0:T(4,128)} %fout.1, s32[3]{0:T(128)} %slot.1, s32[2,256]{1,0:T(2,128)} %bitcast.11, f32[5,512,256]{2,1,0:T(8,128)} %bitcast.8, f32[3,5,512,128]{3,2,1,0:T(8,128)} %bitcast.6, f32[3,3,512,128]{3,2,1,0:T(8,128)} %bitcast.10, ...), custom_call_target="tpu_custom_call" | custom-call | tf_op jit(solution)/shard_map/advance/pallas_call | solution.py:673
  93.2 0.0 copy-start
  93.2 3.8 %copy.15 = f32[5,32,16,256]{3,2,1,0:T(8,128)} copy(f32[5,32,16,256]{3,2,1,0:T(8,128)} %bitcast.9) | data formatting | bytes 5242880
  97.0 0.0 copy-done
  97.0 1.9 %copy.16 = f32[3,5,8,64,128]{4,3,2,1,0:T(8,128)} copy(f32[3,5,8,64,128]{4,3,2,1,0:T(8,128)S(1)} %bitcast.7) | data formatting | bytes 7864320
Async XLA Ops:
  93.2 3.8 %copy-start = (f32[3,5,512,128]{3,2,1,0:T(8,128)S(1)}, f32[3,5,512,128]{3,2,1,0:T(8,128)}, u32[]{:S(2)}) copy-start(f32[3,5,512,128]{3,2,1,0:T(8,128)} %get-tuple-element.5) | copy-start | bytes 11796484

commit v4 on v3

--- a/solution.py
+++ b/solution.py
@@ -614,7 +614,7 @@
         outs = []
         for s in range(BCAP):
             middle(s)
-            if s == 1 and not final:
+            if s == 0 and not final:
                 send_parcels(st + 1)
             if final:
                 outs.append(pltpu.make_async_copy(un.at[s], near_out.at[s], out_sem.at[2 + s]))

time: 99 us -> 99.6 us (level)
  no operation moved by 1% of the time
where the time goes in v4:
time: 99.6 us; the launch traced here: 99.4 us
  Pallas kernels  93.1 us (93%)
  local copies, waits for them, and re-layouts  5.7 us (6%)
    pallas_call x1, Pallas kernels, advance(): pl.pallas_call(main_kernel, out_shape=(jax.ShapeDtypeStruct((5, 512, 256)...  93.1 us
    unnamed x4, local copies, waits for them, and re-layouts  5.7 us

profile of v4, /device:TPU:6, one launch (start us, length us, event | category | flops | bytes accessed | tf_op | source)
XLA Modules:
  0.0 99.4 jit_solution(15224222760840636098)
XLA Ops:
  0.6 93.1 %advance.1 = (f32[5,512,256]{2,1,0:T(8,128)}, f32[3,5,512,128]{3,2,1,0:T(8,128)}) custom-call(s32[3,8]{1,0:T(4,128)} %fin.1, s32[3,8]{1,0:T(4,128)} %fout.1, s32[3]{0:T(128)} %slot.1, s32[2,256]{1,0:T(2,128)} %bitcast.11, f32[5,512,256]{2,1,0:T(8,128)} %bitcast.8, f32[3,5,512,128]{3,2,1,0:T(8,128)} %bitcast.6, f32[3,3,512,128]{3,2,1,0:T(8,128)} %bitcast.10, ...), custom_call_target="tpu_custom_call" | custom-call | tf_op jit(solution)/shard_map/advance/pallas_call | solution.py:673
  93.7 0.0 copy-start
  93.7 3.8 %copy.15 = f32[5,32,16,256]{3,2,1,0:T(8,128)} copy(f32[5,32,16,256]{3,2,1,0:T(8,128)} %bitcast.9) | data formatting | bytes 5242880
  97.5 0.0 copy-done
  97.5 1.9 %copy.16 = f32[3,5,8,64,128]{4,3,2,1,0:T(8,128)} copy(f32[3,5,8,64,128]{4,3,2,1,0:T(8,128)S(1)} %bitcast.7) | data formatting | bytes 7864320
Async XLA Ops:
  93.7 3.8 %copy-start = (f32[3,5,512,128]{3,2,1,0:T(8,128)S(1)}, f32[3,5,512,128]{3,2,1,0:T(8,128)}, u32[]{:S(2)}) copy-start(f32[3,5,512,128]{3,2,1,0:T(8,128)} %get-tuple-element.5) | copy-start | bytes 11796484
